TPU v7x, 256 devices: a whole 4x4x8 slice. The times are simulated.
256 devices in a mesh: grp: 8 (over z), row: 32 (over x, y, core).
Axes of the slice: x: 4, y: 4, z: 8, core: 2. Of those that a mesh axis runs over, the one named last changes fastest.
Arguments:
- basis: float32 [65536, 1024], P(('grp', 'row')), may hold values from -40 to 40
- block: float32 [65536, 512], P(('grp', 'row')), may hold values from -600 to 600
- counts: int32 [8, 32], P('grp', 'row'), may hold values from 128 to 256, as said below
Outputs:
- new_block: float32 [65536, 512], P(('grp', 'row'))
- factor: float32 [512, 512], replicated
Inputs may be any that keep to these rules, and one draw needn't show every extreme that they name: `counts`: each device's live rows are a multiple of 128, at most 256; one device holds exactly 256.
All inputs are finite; a program needn't handle non-finite values.
Results may differ from a plain program's by a relative error of at most 0.0003.
Values sent between devices are 32-bit elements; how exact they have to be, the bound alone decides.
No kernel may reach another device: no remote copies, remote signals or barrier semaphores. Data moves between devices by JAX's collectives and lax.ppermute only.
A program may use at most 64 MiB of HBM per device.

v0:
```python
import functools

import jax
import jax.numpy as jnp
from jax import lax
from jax.experimental import pallas as pl
from jax.experimental.pallas import tpu as pltpu
from jax.sharding import Mesh
from jax.sharding import PartitionSpec as P

ROW = ("row_0", "row_1", "row_2")
GRP_ROW = ("grp", "row_0", "row_1", "row_2")
PLANE = ("row_0", "row_1")

BLOCK = 128
PANEL = 8
HIGHEST = lax.Precision.HIGHEST


def dot_tn(a, b):
    return lax.dot_general(
        a, b, (((0,), (0,)), ((), ())), precision=HIGHEST, preferred_element_type=jnp.float32
    )


def dot_nn(a, b):
    return jnp.dot(a, b, precision=HIGHEST, preferred_element_type=jnp.float32)


def dot_nt(a, b):
    return lax.dot_general(
        a, b, (((1,), (1,)), ((), ())), precision=HIGHEST, preferred_element_type=jnp.float32
    )


def identity(n):
    return (
        lax.broadcasted_iota(jnp.int32, (n, n), 0) == lax.broadcasted_iota(jnp.int32, (n, n), 1)
    ).astype(jnp.float32)


def eliminate_block(d):
    n = BLOCK
    for b in range(0, n, PANEL):
        ra = [d[b + i : b + i + 1, 0:n] for i in range(PANEL)]
        re = [d[b + i : b + i + 1, n : 2 * n] for i in range(PANEL)]
        s = {}
        for i in range(PANEL):
            for j in range(i, PANEL):
                s[i, j] = jnp.broadcast_to(ra[i][:, b + j : b + j + 1], (1, n))
        for k in range(PANEL):
            inv = lax.rsqrt(s[k, k])
            ra[k] = ra[k] * inv
            re[k] = re[k] * inv
            r = [s[k, j] * inv if j > k else None for j in range(PANEL)]
            for i in range(k + 1, PANEL):
                for j in range(i, PANEL):
                    s[i, j] = s[i, j] - r[i] * r[j]
                ra[i] = ra[i] - r[i] * ra[k]
                re[i] = re[i] - r[i] * re[k]
            d[b + k : b + k + 1, 0:n] = ra[k]
            d[b + k : b + k + 1, n : 2 * n] = re[k]
        nxt = b + PANEL
        if nxt >= n:
            continue
        for i in range(PANEL):
            row = slice(nxt + i, nxt + i + 1)
            na, ne = d[row, 0:n], d[row, n : 2 * n]
            for k in range(PANEL):
                c = jnp.broadcast_to(ra[k][:, nxt + i : nxt + i + 1], (1, n))
                na = na - c * ra[k]
                ne = ne - c * re[k]
            d[row, 0:n] = na
            d[row, n : 2 * n] = ne
        far = nxt + PANEL
        if far < n:
            y = d[b : b + PANEL, :]
            d[far:n, :] = d[far:n, :] - dot_tn(y[:, far:n], y)


def split(x):
    hi = x.astype(jnp.bfloat16)
    return hi, (x - hi.astype(jnp.float32)).astype(jnp.bfloat16)


def dot3(a, b):
    ah, al = a
    bh, bl = b

    def one(p, q):
        return jnp.dot(p, q, preferred_element_type=jnp.float32)

    return one(ah, bh) + (one(ah, bl) + one(al, bh))


def rows_of(pair, start, stop):
    return tuple(p[start:stop, :] for p in pair)


def columns_of(pair, start, stop):
    return tuple(p[:, start:stop] for p in pair)


def upper_pairs(n):
    return [(i, j) for i in range(n) for j in range(i, n)]


def masked(ref, count):
    rows = lax.broadcasted_iota(jnp.int32, ref.shape, 0)
    return jnp.where(rows < count, ref[...], 0.0)


def put_by_core(core, keep_ref, send_ref, half, place, tile):
    @pl.when(core == half)
    def _():
        keep_ref[place] = tile

    @pl.when(core != half)
    def _():
        send_ref[place] = tile


def products_kernel(scalars, basis_ref, block_ref, keep_ref, send_ref, *, weight):
    count, core = scalars[0], scalars[1]
    basis = masked(basis_ref, count)
    block = masked(block_ref, count)
    turned = split(jnp.transpose(basis * weight))
    basis = split(basis)
    block = split(block)
    m, k = basis_ref.shape[1] // BLOCK, block_ref.shape[1] // BLOCK
    half_size = keep_ref.shape[0]
    position = 0
    for i in range(m):
        left = rows_of(turned, i * BLOCK, (i + 1) * BLOCK)
        own = dot3(left, columns_of(basis, i * BLOCK, m * BLOCK))
        cross = dot3(left, block)
        tiles = [own[:, j * BLOCK : (j + 1) * BLOCK] for j in range(m - i)]
        tiles += [cross[:, j * BLOCK : (j + 1) * BLOCK] for j in range(k)]
        for tile in tiles:
            put_by_core(
                core, keep_ref, send_ref, position // half_size, position % half_size, tile
            )
            position += 1


def residual_kernel(
    scalars, own_ref, other_ref, basis_ref, block_ref, residual_ref, keep_ref, send_ref,
    s_hi, s_lo, *, weight
):
    count, core = scalars[0], scalars[1]
    m, k = basis_ref.shape[1] // BLOCK, block_ref.shape[1] // BLOCK
    half_size = own_ref.shape[0]
    first = core == 0

    def tile_at(position):
        mine, theirs = own_ref[position % half_size], other_ref[position % half_size]
        swap = first if position < half_size else jnp.logical_not(first)
        return jnp.where(swap, mine, theirs)

    position = 0
    coeffs = []
    eye = identity(BLOCK)
    for i in range(m):
        for j in range(i, m):
            tile = -tile_at(position)
            position += 1
            if i == j:
                tile = eye + tile
            hi, lo = split(tile)
            s_hi[i * BLOCK : (i + 1) * BLOCK, j * BLOCK : (j + 1) * BLOCK] = hi
            s_lo[i * BLOCK : (i + 1) * BLOCK, j * BLOCK : (j + 1) * BLOCK] = lo
            if i != j:
                hi, lo = split(jnp.transpose(tile))
                s_hi[j * BLOCK : (j + 1) * BLOCK, i * BLOCK : (i + 1) * BLOCK] = hi
                s_lo[j * BLOCK : (j + 1) * BLOCK, i * BLOCK : (i + 1) * BLOCK] = lo
        row = []
        for j in range(k):
            row.append(tile_at(position))
            position += 1
        coeffs.append(jnp.concatenate(row, axis=1))
    coeffs = jnp.concatenate(coeffs, axis=0)
    total = coeffs + dot3((s_hi[...], s_lo[...]), split(coeffs))
    basis = split(masked(basis_ref, count))
    residual = masked(block_ref, count) - dot3(basis, split(total))
    residual_ref[...] = residual
    turned = split(jnp.transpose(residual * weight))
    residual = split(residual)
    half_size = keep_ref.shape[0]
    position = 0
    for i in range(k):
        row = dot3(
            rows_of(turned, i * BLOCK, (i + 1) * BLOCK), columns_of(residual, i * BLOCK, k * BLOCK)
        )
        for j in range(k - i):
            put_by_core(
                core, keep_ref, send_ref, position // half_size, position % half_size,
                row[:, j * BLOCK : (j + 1) * BLOCK],
            )
            position += 1


def factor_kernel(scalars, own_ref, other_ref, residual_ref, new_ref, factor_ref, w, d):
    size = residual_ref.shape[1]
    first = scalars[1] == 0
    half_size = own_ref.shape[0]
    w[:, size : 2 * size] = identity(size)
    for position, (i, j) in enumerate(upper_pairs(size // BLOCK)):
        swap = first if position < half_size else jnp.logical_not(first)
        w[i * BLOCK : (i + 1) * BLOCK, j * BLOCK : (j + 1) * BLOCK] = jnp.where(
            swap, own_ref[position % half_size], other_ref[position % half_size]
        )

    def outer(k, carry):
        o = pl.multiple_of(k * BLOCK, BLOCK)
        d[:, 0:BLOCK] = w[pl.ds(o, BLOCK), pl.ds(o, BLOCK)]
        d[:, BLOCK : 2 * BLOCK] = identity(BLOCK)
        eliminate_block(d)
        w[pl.ds(o, BLOCK), :] = dot_nn(d[:, BLOCK : 2 * BLOCK], w[pl.ds(o, BLOCK), :])
        w[pl.ds(o, BLOCK), pl.ds(o, BLOCK)] = d[:, 0:BLOCK]

        def inner(i, c):
            q = pl.multiple_of(i * BLOCK, BLOCK)
            w[pl.ds(q, BLOCK), :] = w[pl.ds(q, BLOCK), :] - dot_tn(
                w[pl.ds(o, BLOCK), pl.ds(q, BLOCK)], w[pl.ds(o, BLOCK), :]
            )
            return c

        return lax.fori_loop(k + 1, size // BLOCK, inner, carry)

    lax.fori_loop(0, size // BLOCK, outer, 0)
    upper = lax.broadcasted_iota(jnp.int32, (size, size), 0) <= lax.broadcasted_iota(
        jnp.int32, (size, size), 1
    )
    factor_ref[...] = jnp.where(upper, w[:, 0:size], 0.0)
    new_ref[...] = dot_nt(residual_ref[...], w[:, size : 2 * size])


def call(kernel, out_shapes, scratch, name):
    def run(scalars, *arrays):
        vmem = pl.BlockSpec(memory_space=pltpu.VMEM)
        return pl.pallas_call(
            kernel,
            out_shape=[jax.ShapeDtypeStruct(s, jnp.float32) for s in out_shapes],
            in_specs=[pl.BlockSpec(memory_space=pltpu.SMEM)] + [vmem] * len(arrays),
            out_specs=[vmem] * len(out_shapes),
            scratch_shapes=scratch,
            compiler_params=pltpu.CompilerParams(vmem_limit_bytes=48 << 20),
            name=name,
        )(scalars, *arrays)

    return run


def swap_cores(x):
    return lax.ppermute(x, "row_2", [(0, 1), (1, 0)])


def exchange(x, axes):
    return lax.all_to_all(x, axes, 0, 0, tiled=True)


def to_all(x, axes):
    count = lax.axis_size(axes)
    return exchange(jnp.broadcast_to(x[None], (count, *x.shape)), axes)


def sum_halves(keep, send, spread):
    total = (keep + swap_cores(send)).reshape(-1, 8, 128)
    plane = lax.axis_size(PLANE)
    part = jnp.sum(exchange(total.reshape(plane, -1, 8, 128), PLANE), axis=0)
    if spread:
        grp = lax.axis_size("grp")
        lines = part.shape[0]
        padded = jnp.pad(part, ((0, -lines % grp), (0, 0), (0, 0)))
        part = jnp.sum(exchange(padded.reshape(grp, -1, 8, 128), "grp"), axis=0)
        part = to_all(part, "grp").reshape(-1, 8, 128)[:lines]
    else:
        part = jnp.sum(to_all(part, "grp"), axis=0)
    whole = to_all(part, PLANE).reshape(keep.shape)
    return whole, swap_cores(whole)


def body(basis, block, counts):
    row_slots, size = block.shape
    m, k = basis.shape[1] // BLOCK, size // BLOCK
    devices = lax.axis_size("grp") * lax.axis_size(ROW)
    weight = 1.0 / (row_slots * devices)
    scalars = jnp.stack([counts[0, 0], lax.axis_index("row_2").astype(jnp.int32)])
    tiles = (m * (m + 1) // 2 + m * k) // 2
    gram_tiles = k * (k + 1) // 4
    half = (tiles, BLOCK, BLOCK)
    gram_half = (gram_tiles, BLOCK, BLOCK)
    keep, send = call(
        functools.partial(products_kernel, weight=weight), [half, half], [], "products"
    )(scalars, basis, block)
    own, other = sum_halves(keep, send, True)
    wide = pltpu.VMEM((m * BLOCK, m * BLOCK), jnp.bfloat16)
    residual, keep, send = call(
        functools.partial(residual_kernel, weight=weight),
        [block.shape, gram_half, gram_half],
        [wide, wide],
        "residual",
    )(scalars, own, other, basis, block)
    own, other = sum_halves(keep, send, False)
    new_block, factor = call(
        factor_kernel,
        [block.shape, (size, size)],
        [
            pltpu.VMEM((size, 2 * size), jnp.float32),
            pltpu.VMEM((BLOCK, 2 * BLOCK), jnp.float32),
        ],
        "factor",
    )(scalars, own, other, residual)
    return new_block, factor


def solution(mesh):
    torus = Mesh(
        mesh.devices.reshape(mesh.shape["grp"], 4, 4, 2), ("grp", "row_0", "row_1", "row_2")
    )
    in_specs = (P(GRP_ROW, None), P(GRP_ROW, None), P("grp", ROW))
    out_specs = (P(GRP_ROW, None), P())
    return jax.shard_map(body, mesh=torus, in_specs=in_specs, out_specs=out_specs, check_vma=False)
```

profile of v0, /device:TPU:1, one launch (start us, length us, event | category | flops | bytes accessed | tf_op | source)
XLA Modules:
  0.0 191.6 jit_solution(9390753387876777147)
XLA Ops:
  1.3 0.1 pad_add_fusion.scalars
  1.4 0.0 copy-start
  1.4 1.2 copy-done
  2.6 0.0 copy-start.2
  2.6 1.0 copy-done.2
  3.6 4.6 %products.1 = (f32[34,128,128]{2,1,0:T(8,128)S(1)}, f32[34,128,128]{2,1,0:T(8,128)S(1)}) custom-call(s32[2]{0:T(128)S(1)} %pad_add_fusion.scalars, f32[256,1024]{1,0:T(8,128)S(1)} %copy-done, f32[256,512]{1,0:T(8,128)S(1)} %copy-done.2), custom_call_target="tpu_custom_call" | custom-call | tf_op jit(solution)/shard_map/products/pallas_call | solution.py:241
  8.2 3.3 %collective-permute-start = (f32[34,128,128]{2,1,0:T(8,128)S(1)}, f32[34,128,128]{2,1,0:T(8,128)S(1)}, u32[]{:S(2)}, u32[]{:S(2)}) collective-permute-start(f32[34,128,128]{2,1,0:T(8,128)S(1)} %get-tuple-element.8), channel_id=1, source_target_pairs={{0,1},{1,0},{2,3},{3,2},{4,5},{5,4},{6,7},{7,6},{8,9},{9,8},{10,11... | collective-permute-start | bytes 6684680 | tf_op jit(solution)/shard_map/ppermute | solution.py:255
  11.5 4.0 %collective-permute-done = f32[34,128,128]{2,1,0:T(8,128)S(1)} collective-permute-done((f32[34,128,128]{2,1,0:T(8,128)S(1)}, f32[34,128,128]{2,1,0:T(8,128)S(1)}, u32[]{:S(2)}, u32[]{:S(2)}) %collective-permute-start) | collective-permute-done | bytes 2228256 | tf_op jit(solution)/shard_map/ppermute | solution.py:255
  15.5 0.4 add.8
  15.9 33.7 %all_to_all.35 = f32[16,34,8,128]{3,2,1,0:T(8,128)S(1)} all-to-all(f32[16,34,8,128]{3,2,1,0:T(8,128)S(1)} %bitcast.13), channel_id=1, replica_groups=mesh['grp'=8,'row_0'=4,'row_1'=4,'row_2'=2] {'row_0','row_1'}, dimensions={0} | all-to-all | bytes 4456448 | tf_op jit(solution)/shard_map/all_to_all | solution.py:259
  49.6 0.1 reduce_sum.36
  49.7 16.3 %all_to_all.36 = f32[8,5,8,128]{3,2,1,0:T(8,128)S(1)} all-to-all(f32[8,5,8,128]{3,2,1,0:T(8,128)S(1)} %bitcast.15), channel_id=1, replica_groups=mesh['grp'=8,'row_0'=4,'row_1'=4,'row_2'=2] {'grp'}, dimensions={0} | all-to-all | bytes 327680 | tf_op jit(solution)/shard_map/all_to_all | solution.py:259
  66.0 10.7 %all_to_all.37 = f32[8,5,8,128]{3,2,1,0:T(8,128)S(1)} all-to-all(f32[8,5,8,128]{3,2,1,0:T(8,128)S(1)} %broadcast_in_dim.8), channel_id=1, replica_groups=mesh['grp'=8,'row_0'=4,'row_1'=4,'row_2'=2] {'grp'}, dimensions={0} | all-to-all | bytes 327680 | tf_op jit(solution)/shard_map/all_to_all | solution.py:259
  76.7 0.1 broadcast_in_dim.9
  76.9 0.0 copy-start.1
  76.9 0.0 copy-start.3
  76.9 28.6 %all_to_all.38 = f32[16,34,8,128]{3,2,1,0:T(8,128)S(1)} all-to-all(f32[16,34,8,128]{3,2,1,0:T(8,128)S(1)} %broadcast_in_dim.9), channel_id=1, replica_groups=mesh['grp'=8,'row_0'=4,'row_1'=4,'row_2'=2] {'row_0','row_1'}, dimensions={0} | all-to-all | bytes 4456448 | tf_op jit(solution)/shard_map/all_to_all | solution.py:259
  105.5 5.5 %collective-permute-start.1 = (f32[34,128,128]{2,1,0:T(8,128)S(1)}, f32[34,128,128]{2,1,0:T(8,128)S(1)}, u32[]{:S(2)}, u32[]{:S(2)}) collective-permute-start(f32[34,128,128]{2,1,0:T(8,128)S(1)} %bitcast.9), channel_id=1, source_target_pairs={{0,1},{1,0},{2,3},{3,2},{4,5},{5,4},{6,7},{7,6},{8,9},{9,8},{10,11... | collective-permute-start | bytes 6684680 | tf_op jit(solution)/shard_map/ppermute | solution.py:255
  110.9 4.0 %collective-permute-done.1.other_ref = f32[34,128,128]{2,1,0:T(8,128)S(1)} collective-permute-done((f32[34,128,128]{2,1,0:T(8,128)S(1)}, f32[34,128,128]{2,1,0:T(8,128)S(1)}, u32[]{:S(2)}, u32[]{:S(2)}) %collective-permute-start.1) | collective-permute-done | bytes 2228256 | tf_op jit(solution)/shard_map/ppermute | solution.py:255
  114.9 0.0 copy-start.4
  114.9 1.4 copy-done.4
  116.3 0.0 copy-done.1
  116.3 0.0 copy-done.3
  116.3 7.5 %residual.1 = (f32[256,512]{1,0:T(8,128)S(1)}, f32[5,128,128]{2,1,0:T(8,128)S(1)}, f32[5,128,128]{2,1,0:T(8,128)S(1)}) custom-call(s32[2]{0:T(128)S(1)} %pad_add_fusion.scalars, f32[34,128,128]{2,1,0:T(8,128)S(1)} %bitcast.10, f32[34,128,128]{2,1,0:T(8,128)} %copy-done.4, f32[256,1024]{1,0:T(8,128)S(1)} %copy-done.1, f32[256,512]{1,0:T(8,128)S(1)} %copy-done.3), custom_call_target="tpu_custom_call" | custom-call | tf_op jit(solution)/shard_map/residual/pallas_call | solution.py:241
  123.8 0.5 collective-permute-start.2
  124.3 1.3 collective-permute-done.2
  125.6 11.1 %all_to_all.39 = f32[16,5,8,128]{3,2,1,0:T(8,128)S(1)} all-to-all(f32[16,5,8,128]{3,2,1,0:T(8,128)S(1)} %bitcast.14), channel_id=1, replica_groups=mesh['grp'=8,'row_0'=4,'row_1'=4,'row_2'=2] {'row_0','row_1'}, dimensions={0} | all-to-all | bytes 655360 | tf_op jit(solution)/shard_map/all_to_all | solution.py:259
  136.7 10.8 %all_to_all.40 = f32[8,5,8,128]{3,2,1,0:T(8,128)S(1)} all-to-all(f32[8,5,8,128]{3,2,1,0:T(8,128)S(1)} %broadcast_in_dim.10), channel_id=1, replica_groups=mesh['grp'=8,'row_0'=4,'row_1'=4,'row_2'=2] {'grp'}, dimensions={0} | all-to-all | bytes 327680 | tf_op jit(solution)/shard_map/all_to_all | solution.py:259
  147.5 11.5 %all_to_all.41 = f32[16,5,8,128]{3,2,1,0:T(8,128)S(1)} all-to-all(f32[16,5,8,128]{3,2,1,0:T(8,128)S(1)} %broadcast_in_dim.11), channel_id=1, replica_groups=mesh['grp'=8,'row_0'=4,'row_1'=4,'row_2'=2] {'row_0','row_1'}, dimensions={0} | all-to-all | bytes 655360 | tf_op jit(solution)/shard_map/all_to_all | solution.py:259
  159.0 4.0 %collective-permute-start.3 = (f32[5,128,128]{2,1,0:T(8,128)S(1)}, f32[5,128,128]{2,1,0:T(8,128)S(1)}, u32[]{:S(2)}, u32[]{:S(2)}) collective-permute-start(f32[5,128,128]{2,1,0:T(8,128)S(1)} %bitcast.11), channel_id=1, source_target_pairs={{0,1},{1,0},{2,3},{3,2},{4,5},{5,4},{6,7},{7,6},{8,9},{9,8},{10,11... | collective-permute-start | bytes 983048 | tf_op jit(solution)/shard_map/ppermute | solution.py:255
  163.0 1.3 collective-permute-done.3.other_ref
  164.3 27.4 %factor.1 = (f32[256,512]{1,0:T(8,128)}, f32[512,512]{1,0:T(8,128)}) custom-call(s32[2]{0:T(128)S(1)} %pad_add_fusion.scalars, f32[5,128,128]{2,1,0:T(8,128)S(1)} %bitcast.12, f32[5,128,128]{2,1,0:T(8,128)S(1)} %collective-permute-done.3.other_ref, f32[256,512]{1,0:T(8,128)S(1)} %get-tuple-element.11.residual_ref), custom_call_target="tpu_custom_call" | custom-call | tf_op jit(solution)/shard_map/factor/pallas_call | solution.py:241
  (9 shorter events, 0.2 us)
Async XLA Ops:
  1.4 1.2 copy-start
  2.6 1.0 copy-start.2
  8.2 7.3 %collective-permute-start = (f32[34,128,128]{2,1,0:T(8,128)S(1)}, f32[34,128,128]{2,1,0:T(8,128)S(1)}, u32[]{:S(2)}, u32[]{:S(2)}) collective-permute-start(f32[34,128,128]{2,1,0:T(8,128)S(1)} %get-tuple-element.8), channel_id=1, source_target_pairs={{0,1},{1,0},{2,3},{3,2},{4,5},{5,4},{6,7},{7,6},{8,9},{9,8},{10,11... | collective-permute-start | bytes 6684680 | tf_op jit(solution)/shard_map/ppermute | solution.py:255
  76.9 39.4 %copy-start.1 = (f32[256,1024]{1,0:T(8,128)S(1)}, f32[256,1024]{1,0:T(8,128)}, u32[]{:S(2)}) copy-start(f32[256,1024]{1,0:T(8,128)} %basis_ref.3) | copy-start | bytes 3145732
  76.9 39.4 %copy-start.3 = (f32[256,512]{1,0:T(8,128)S(1)}, f32[256,512]{1,0:T(8,128)}, u32[]{:S(2)}) copy-start(f32[256,512]{1,0:T(8,128)} %block_ref.3) | copy-start | bytes 1572868
  105.5 9.4 %collective-permute-start.1 = (f32[34,128,128]{2,1,0:T(8,128)S(1)}, f32[34,128,128]{2,1,0:T(8,128)S(1)}, u32[]{:S(2)}, u32[]{:S(2)}) collective-permute-start(f32[34,128,128]{2,1,0:T(8,128)S(1)} %bitcast.9), channel_id=1, source_target_pairs={{0,1},{1,0},{2,3},{3,2},{4,5},{5,4},{6,7},{7,6},{8,9},{9,8},{10,11... | collective-permute-start | bytes 6684680 | tf_op jit(solution)/shard_map/ppermute | solution.py:255
  114.9 1.4 copy-start.4
  123.8 1.7 collective-permute-start.2
  159.0 5.2 %collective-permute-start.3 = (f32[5,128,128]{2,1,0:T(8,128)S(1)}, f32[5,128,128]{2,1,0:T(8,128)S(1)}, u32[]{:S(2)}, u32[]{:S(2)}) collective-permute-start(f32[5,128,128]{2,1,0:T(8,128)S(1)} %bitcast.11), channel_id=1, source_target_pairs={{0,1},{1,0},{2,3},{3,2},{4,5},{5,4},{6,7},{7,6},{8,9},{9,8},{10,11... | collective-permute-start | bytes 983048 | tf_op jit(solution)/shard_map/ppermute | solution.py:255
where the time goes:
time: 192 us
  blocking collectives  123 us (64%)
  Pallas kernels  39.5 us (21%)
  starting transfers between devices  13.2 us (7%)
  waiting for transfers between devices  10.5 us (5%)
  local copies, waits for them, and re-layouts  3.88 us (2%)
    all_to_all x7, blocking collectives, exchange(): return lax.all_to_all(x, axes, 0, 0, tiled=True)  123 us
    pallas_call x3, Pallas kernels, run(): pl.pallas_call(kernel, out_shape=[jax.ShapeDtypeStruct(s, jnp.float32) fo...  39.5 us
    ppermute x4, starting transfers between devices, swap_cores(): return lax.ppermute(x, 'row_2', [(0, 1), (1, 0)])  13.2 us
    ppermute x4, waiting for transfers between devices, swap_cores(): return lax.ppermute(x, 'row_2', [(0, 1), (1, 0)])  10.5 us
  transfers between devices with their start and end apart: 4, of which 4 were waited for; matrix products, arithmetic and copies ran while one was open for 0% of the time, Pallas kernels for 0%

commit v1 on v0

--- a/solution.py
+++ b/solution.py
@@ -13,24 +13,9 @@
 PLANE = ("row_0", "row_1")
 
 BLOCK = 128
+STEP = 64
 PANEL = 8
 HIGHEST = lax.Precision.HIGHEST
-
-
-def dot_tn(a, b):
-    return lax.dot_general(
-        a, b, (((0,), (0,)), ((), ())), precision=HIGHEST, preferred_element_type=jnp.float32
-    )
-
-
-def dot_nn(a, b):
-    return jnp.dot(a, b, precision=HIGHEST, preferred_element_type=jnp.float32)
-
-
-def dot_nt(a, b):
-    return lax.dot_general(
-        a, b, (((1,), (1,)), ((), ())), precision=HIGHEST, preferred_element_type=jnp.float32
-    )
 
 
 def identity(n):
@@ -39,43 +24,85 @@
     ).astype(jnp.float32)
 
 
-def eliminate_block(d):
-    n = BLOCK
-    for b in range(0, n, PANEL):
-        ra = [d[b + i : b + i + 1, 0:n] for i in range(PANEL)]
-        re = [d[b + i : b + i + 1, n : 2 * n] for i in range(PANEL)]
-        s = {}
-        for i in range(PANEL):
-            for j in range(i, PANEL):
-                s[i, j] = jnp.broadcast_to(ra[i][:, b + j : b + j + 1], (1, n))
-        for k in range(PANEL):
-            inv = lax.rsqrt(s[k, k])
-            ra[k] = ra[k] * inv
-            re[k] = re[k] * inv
-            r = [s[k, j] * inv if j > k else None for j in range(PANEL)]
-            for i in range(k + 1, PANEL):
-                for j in range(i, PANEL):
-                    s[i, j] = s[i, j] - r[i] * r[j]
-                ra[i] = ra[i] - r[i] * ra[k]
-                re[i] = re[i] - r[i] * re[k]
-            d[b + k : b + k + 1, 0:n] = ra[k]
-            d[b + k : b + k + 1, n : 2 * n] = re[k]
-        nxt = b + PANEL
-        if nxt >= n:
-            continue
-        for i in range(PANEL):
-            row = slice(nxt + i, nxt + i + 1)
-            na, ne = d[row, 0:n], d[row, n : 2 * n]
-            for k in range(PANEL):
-                c = jnp.broadcast_to(ra[k][:, nxt + i : nxt + i + 1], (1, n))
-                na = na - c * ra[k]
-                ne = ne - c * re[k]
-            d[row, 0:n] = na
-            d[row, n : 2 * n] = ne
-        far = nxt + PANEL
-        if far < n:
-            y = d[b : b + PANEL, :]
-            d[far:n, :] = d[far:n, :] - dot_tn(y[:, far:n], y)
+def spread(x):
+    return jnp.broadcast_to(x, (PANEL, BLOCK))
+
+
+def tree_sum(terms):
+    while len(terms) > 1:
+        terms = [a + b for a, b in zip(terms[::2], terms[1::2])]
+    return terms[0]
+
+
+def eliminate(v, a0):
+    n = len(v)
+    row = lax.broadcasted_iota(jnp.int32, (PANEL, BLOCK), 0)
+    panel = range(PANEL)
+    diag = [spread(v[0][:, a0 + j : a0 + j + 1]) for j in panel]
+    for p in range(n):
+        base = a0 + PANEL * p
+        turned = {
+            q: [spread(v[q][:, base + j : base + j + 1]) for j in panel] for q in range(p + 1, n)
+        }
+        if p + 1 < n:
+            after = base + PANEL
+            ahead = [spread(v[p + 1][:, after + j : after + j + 1]) for j in panel]
+        current = v[p]
+        rows, coefs, inverses = [], [], []
+        scale = None
+        for k in panel:
+            inv = lax.rsqrt(spread(diag[k][k : k + 1, :]))
+            col = diag[k] * inv
+            r = [spread(col[j : j + 1, :]) if j > k else None for j in panel]
+            for j in range(k + 1, PANEL):
+                diag[j] = diag[j] - col * r[j]
+            own = spread(current[k : k + 1, :]) * inv
+            rows.append(own)
+            if k < PANEL - 1:
+                current = current - jnp.where(row > k, col, 0.0) * own
+            scale = inv if scale is None else jnp.where(row >= k, inv, scale)
+            coefs.append(r)
+            inverses.append(inv)
+        v[p] = current * scale
+        for q in range(p + 1, n):
+            t = turned[q]
+            for k in panel:
+                t[k] = t[k] * inverses[k]
+                for j in range(k + 1, PANEL):
+                    t[j] = t[j] - t[k] * coefs[k][j]
+            v[q] = v[q] - tree_sum([t[k] * rows[k] for k in panel])
+            if q == p + 1:
+                diag = [
+                    ahead[j] - tree_sum([t[k] * spread(t[k][j : j + 1, :]) for k in panel])
+                    for j in panel
+                ]
+    return v
+
+
+def twice_left(x):
+    hi, lo = split(x)
+    lane = lax.broadcasted_iota(jnp.int32, x.shape, 1)
+    both = jnp.where(lane < STEP, hi.astype(jnp.float32), lo.astype(jnp.float32))
+    both = both.astype(jnp.bfloat16)
+    return jnp.concatenate([both, both], axis=1)
+
+
+def stacked_dot(left4, x):
+    hi, lo = split(x)
+    return jnp.dot(
+        left4, jnp.concatenate([hi, hi, lo, lo], axis=0), preferred_element_type=jnp.float32
+    )
+
+
+def stacked_dot_tn(a, b):
+    ah, al = split(a)
+    bh, bl = split(b)
+    return lax.dot_general(
+        jnp.concatenate([ah, al, ah, al], axis=0),
+        jnp.concatenate([bh, bh, bl, bl], axis=0),
+        (((0,), (0,)), ((), ())),
+        preferred_element_type=jnp.float32,
+    )
 
 
 def split(x):
@@ -134,7 +161,13 @@
         left = rows_of(turned, i * BLOCK, (i + 1) * BLOCK)
         own = dot3(left, columns_of(basis, i * BLOCK, m * BLOCK))
         cross = dot3(left, block)
+        rest = jnp.dot(
+            left[1],
+            basis[1][:, i * BLOCK : (i + 1) * BLOCK],
+            preferred_element_type=jnp.float32,
+        )
         tiles = [own[:, j * BLOCK : (j + 1) * BLOCK] for j in range(m - i)]
+        tiles[0] = tiles[0] + rest
         tiles += [cross[:, j * BLOCK : (j + 1) * BLOCK] for j in range(k)]
         for tile in tiles:
             put_by_core(
@@ -180,8 +213,10 @@
         coeffs.append(jnp.concatenate(row, axis=1))
     coeffs = jnp.concatenate(coeffs, axis=0)
     total = coeffs + dot3((s_hi[...], s_lo[...]), split(coeffs))
-    basis = split(masked(basis_ref, count))
-    residual = masked(block_ref, count) - dot3(basis, split(total))
+    basis = masked(basis_ref, count)
+    residual = masked(block_ref, count) - jnp.dot(
+        basis, total, precision=HIGHEST, preferred_element_type=jnp.float32
+    )
     residual_ref[...] = residual
     turned = split(jnp.transpose(residual * weight))
     residual = split(residual)
@@ -199,40 +234,85 @@
             position += 1
 
 
-def factor_kernel(scalars, own_ref, other_ref, residual_ref, new_ref, factor_ref, w, d):
+def dot3_nt(a, b):
+    ah, al = a
+    bh, bl = b
+
+    def one(p, q):
+        return lax.dot_general(p, q, (((1,), (1,)), ((), ())), preferred_element_type=jnp.float32)
+
+    return one(ah, bh) + (one(ah, bl) + one(al, bh))
+
+
+def factor_kernel(scalars, own_ref, other_ref, residual_ref, new_ref, factor_ref, w, inv_ref):
     size = residual_ref.shape[1]
     first = scalars[1] == 0
     half_size = own_ref.shape[0]
-    w[:, size : 2 * size] = identity(size)
+    zero = jnp.zeros((BLOCK, BLOCK), jnp.float32)
     for position, (i, j) in enumerate(upper_pairs(size // BLOCK)):
         swap = first if position < half_size else jnp.logical_not(first)
         w[i * BLOCK : (i + 1) * BLOCK, j * BLOCK : (j + 1) * BLOCK] = jnp.where(
             swap, own_ref[position % half_size], other_ref[position % half_size]
         )
-
-    def outer(k, carry):
-        o = pl.multiple_of(k * BLOCK, BLOCK)
-        d[:, 0:BLOCK] = w[pl.ds(o, BLOCK), pl.ds(o, BLOCK)]
-        d[:, BLOCK : 2 * BLOCK] = identity(BLOCK)
-        eliminate_block(d)
-        w[pl.ds(o, BLOCK), :] = dot_nn(d[:, BLOCK : 2 * BLOCK], w[pl.ds(o, BLOCK), :])
-        w[pl.ds(o, BLOCK), pl.ds(o, BLOCK)] = d[:, 0:BLOCK]
-
-        def inner(i, c):
-            q = pl.multiple_of(i * BLOCK, BLOCK)
-            w[pl.ds(q, BLOCK), :] = w[pl.ds(q, BLOCK), :] - dot_tn(
-                w[pl.ds(o, BLOCK), pl.ds(q, BLOCK)], w[pl.ds(o, BLOCK), :]
+        if i != j:
+            w[j * BLOCK : (j + 1) * BLOCK, i * BLOCK : (i + 1) * BLOCK] = zero
+    residual = split(residual_ref[...])
+    zero = jnp.zeros((STEP, BLOCK), jnp.float32)
+    lane = lax.broadcasted_iota(jnp.int32, (PANEL, BLOCK), 1)
+    row = lax.broadcasted_iota(jnp.int32, (PANEL, BLOCK), 0)
+    lanes = lax.broadcasted_iota(jnp.int32, (STEP, BLOCK), 1)
+    rows = lax.broadcasted_iota(jnp.int32, (STEP, BLOCK), 0)
+    following = None
+    for k in range(size // STEP):
+        o = k * STEP
+        end = o + STEP
+        lo = o // BLOCK * BLOCK
+        hi = lo + BLOCK
+        a0 = o - lo
+        e0 = STEP - a0
+        square = w[o:end, lo:hi] if following is None else following
+        v = []
+        for q in range(STEP // PANEL):
+            eye = (lane - e0 == row + PANEL * q).astype(jnp.float32)
+            inside = (lane >= a0) & (lane < a0 + STEP)
+            v.append(jnp.where(inside, square[PANEL * q : PANEL * q + PANEL, :], eye))
+        d = jnp.concatenate(eliminate(v, a0), axis=0)
+        swapped = pltpu.roll(d, STEP, 1)
+        here = (lanes >= a0) & (lanes < a0 + STEP)
+        left4 = twice_left(jnp.where(here, swapped, d))
+        if end < size:
+            lo2 = end // BLOCK * BLOCK
+            part = stacked_dot(left4, w[o:end, lo2 : lo2 + BLOCK])
+            drop = stacked_dot_tn(part, part)[end - lo2 : end - lo2 + STEP, :]
+            following = w[end : end + STEP, lo2 : lo2 + BLOCK] - drop
+        z = stacked_dot(left4, w[o:end, :])
+        z_here = z[:, lo:hi]
+        upper = jnp.where(
+            here & (lanes - a0 >= rows), d, jnp.where(lanes >= a0 + STEP, z_here, 0.0)
+        )
+        lower = jnp.where(
+            here, jnp.where(lanes - a0 <= rows, swapped, 0.0), jnp.where(lanes < a0, z_here, 0.0)
+        )
+        for c in range(0, size, BLOCK):
+            band = slice(c, c + BLOCK)
+            factor_ref[o:end, band] = zero if c < lo else (upper if c == lo else z[:, band])
+            inv_ref[o:end, band] = z[:, band] if c < lo else (lower if c == lo else zero)
+        if end < size:
+            pieces = [z[:, :lo]] if lo else []
+            pieces.append(jnp.where(here, swapped, z_here))
+            if hi < size:
+                pieces.append(z[:, hi:])
+            first_lane = end // BLOCK * BLOCK
+            drop = stacked_dot_tn(z[:, first_lane:], jnp.concatenate(pieces, axis=1))
+            column = lax.broadcasted_iota(jnp.int32, (size - end, size), 1)
+            w[end:size, :] = (
+                jnp.where((column >= o) & (column < end), 0.0, w[end:size, :])
+                - drop[end - first_lane :, :]
             )
-            return c
-
-        return lax.fori_loop(k + 1, size // BLOCK, inner, carry)
-
-    lax.fori_loop(0, size // BLOCK, outer, 0)
-    upper = lax.broadcasted_iota(jnp.int32, (size, size), 0) <= lax.broadcasted_iota(
-        jnp.int32, (size, size), 1
-    )
-    factor_ref[...] = jnp.where(upper, w[:, 0:size], 0.0)
-    new_ref[...] = dot_nt(residual_ref[...], w[:, size : 2 * size])
+        if end == hi:
+            new_ref[:, lo:hi] = dot3_nt(
+                columns_of(residual, 0, hi), split(inv_ref[lo:hi, 0:hi])
+            )
 
 
 def call(kernel, out_shapes, scratch, name):
@@ -306,8 +386,8 @@
         factor_kernel,
         [block.shape, (size, size)],
         [
-            pltpu.VMEM((size, 2 * size), jnp.float32),
-            pltpu.VMEM((BLOCK, 2 * BLOCK), jnp.float32),
+            pltpu.VMEM((size, size), jnp.float32),
+            pltpu.VMEM((size, size), jnp.float32),
         ],
         "factor",
     )(scalars, own, other, residual)

time: 192 us -> 180 us (0.938)
  Pallas kernels: 39.5 us -> 26.8 us
    pallas_call x3, Pallas kernels: 39.5 us -> 26.8 us  [run(): pl.pallas_call(kernel, out_shape=[jax.ShapeDtypeStruct(s, jnp.float32) fo...]
where the time goes in v1:
time: 180 us; the launch traced here: 179 us
  blocking collectives  123 us (68%)
  Pallas kernels  26.8 us (15%)
  starting transfers between devices  13.4 us (7%)
  waiting for transfers between devices  10.5 us (6%)
  local copies, waits for them, and re-layouts  3.88 us (2%)
    all_to_all x7, blocking collectives, exchange(): return lax.all_to_all(x, axes, 0, 0, tiled=True)  123 us
    pallas_call x3, Pallas kernels, run(): pl.pallas_call(kernel, out_shape=[jax.ShapeDtypeStruct(s, jnp.float32) fo...  26.8 us
    ppermute x4, starting transfers between devices, swap_cores(): return lax.ppermute(x, 'row_2', [(0, 1), (1, 0)])  13.4 us
    ppermute x4, waiting for transfers between devices, swap_cores(): return lax.ppermute(x, 'row_2', [(0, 1), (1, 0)])  10.5 us
    unnamed x10, local copies, waits for them, and re-layouts  3.67 us
  transfers between devices with their start and end apart: 4, of which 4 were waited for; matrix products, arithmetic and copies ran while one was open for 0% of the time, Pallas kernels for 0%

profile of v1, /device:TPU:1, one launch (start us, length us, event | category | flops | bytes accessed | tf_op | source)
XLA Modules:
  0.0 179.1 jit_solution(11326487184403220000)
XLA Ops:
  1.3 0.1 pad_add_fusion.scalars
  1.4 0.0 copy-start
  1.4 1.2 copy-done
  2.6 0.0 copy-start.2
  2.6 1.0 copy-done.2
  3.6 4.7 %products.1 = (f32[34,128,128]{2,1,0:T(8,128)S(1)}, f32[34,128,128]{2,1,0:T(8,128)S(1)}) custom-call(s32[2]{0:T(128)S(1)} %pad_add_fusion.scalars, f32[256,1024]{1,0:T(8,128)S(1)} %copy-done, f32[256,512]{1,0:T(8,128)S(1)} %copy-done.2), custom_call_target="tpu_custom_call" | custom-call | tf_op jit(solution)/shard_map/products/pallas_call | solution.py:321
  8.3 3.3 %collective-permute-start = (f32[34,128,128]{2,1,0:T(8,128)S(1)}, f32[34,128,128]{2,1,0:T(8,128)S(1)}, u32[]{:S(2)}, u32[]{:S(2)}) collective-permute-start(f32[34,128,128]{2,1,0:T(8,128)S(1)} %get-tuple-element.8), channel_id=1, source_target_pairs={{0,1},{1,0},{2,3},{3,2},{4,5},{5,4},{6,7},{7,6},{8,9},{9,8},{10,11... | collective-permute-start | bytes 6684680 | tf_op jit(solution)/shard_map/ppermute | solution.py:335
  11.7 4.0 %collective-permute-done = f32[34,128,128]{2,1,0:T(8,128)S(1)} collective-permute-done((f32[34,128,128]{2,1,0:T(8,128)S(1)}, f32[34,128,128]{2,1,0:T(8,128)S(1)}, u32[]{:S(2)}, u32[]{:S(2)}) %collective-permute-start) | collective-permute-done | bytes 2228256 | tf_op jit(solution)/shard_map/ppermute | solution.py:335
  15.6 0.4 add.8
  16.0 33.6 %all_to_all.35 = f32[16,34,8,128]{3,2,1,0:T(8,128)S(1)} all-to-all(f32[16,34,8,128]{3,2,1,0:T(8,128)S(1)} %bitcast.13), channel_id=1, replica_groups=mesh['grp'=8,'row_0'=4,'row_1'=4,'row_2'=2] {'row_0','row_1'}, dimensions={0} | all-to-all | bytes 4456448 | tf_op jit(solution)/shard_map/all_to_all | solution.py:339
  49.6 0.1 reduce_sum.36
  49.8 16.3 %all_to_all.36 = f32[8,5,8,128]{3,2,1,0:T(8,128)S(1)} all-to-all(f32[8,5,8,128]{3,2,1,0:T(8,128)S(1)} %bitcast.15), channel_id=1, replica_groups=mesh['grp'=8,'row_0'=4,'row_1'=4,'row_2'=2] {'grp'}, dimensions={0} | all-to-all | bytes 327680 | tf_op jit(solution)/shard_map/all_to_all | solution.py:339
  66.1 10.7 %all_to_all.37 = f32[8,5,8,128]{3,2,1,0:T(8,128)S(1)} all-to-all(f32[8,5,8,128]{3,2,1,0:T(8,128)S(1)} %broadcast_in_dim.8), channel_id=1, replica_groups=mesh['grp'=8,'row_0'=4,'row_1'=4,'row_2'=2] {'grp'}, dimensions={0} | all-to-all | bytes 327680 | tf_op jit(solution)/shard_map/all_to_all | solution.py:339
  76.8 0.1 broadcast_in_dim.9
  77.0 0.0 copy-start.1
  77.0 0.0 copy-start.3
  77.0 28.6 %all_to_all.38 = f32[16,34,8,128]{3,2,1,0:T(8,128)S(1)} all-to-all(f32[16,34,8,128]{3,2,1,0:T(8,128)S(1)} %broadcast_in_dim.9), channel_id=1, replica_groups=mesh['grp'=8,'row_0'=4,'row_1'=4,'row_2'=2] {'row_0','row_1'}, dimensions={0} | all-to-all | bytes 4456448 | tf_op jit(solution)/shard_map/all_to_all | solution.py:339
  105.6 5.5 %collective-permute-start.1 = (f32[34,128,128]{2,1,0:T(8,128)S(1)}, f32[34,128,128]{2,1,0:T(8,128)S(1)}, u32[]{:S(2)}, u32[]{:S(2)}) collective-permute-start(f32[34,128,128]{2,1,0:T(8,128)S(1)} %bitcast.9), channel_id=1, source_target_pairs={{0,1},{1,0},{2,3},{3,2},{4,5},{5,4},{6,7},{7,6},{8,9},{9,8},{10,11... | collective-permute-start | bytes 6684680 | tf_op jit(solution)/shard_map/ppermute | solution.py:335
  111.0 4.0 %collective-permute-done.1.other_ref = f32[34,128,128]{2,1,0:T(8,128)S(1)} collective-permute-done((f32[34,128,128]{2,1,0:T(8,128)S(1)}, f32[34,128,128]{2,1,0:T(8,128)S(1)}, u32[]{:S(2)}, u32[]{:S(2)}) %collective-permute-start.1) | collective-permute-done | bytes 2228256 | tf_op jit(solution)/shard_map/ppermute | solution.py:335
  115.0 0.0 copy-start.4
  115.0 1.4 copy-done.4
  116.4 0.0 copy-done.1
  116.4 0.0 copy-done.3
  116.4 8.5 %residual.1 = (f32[256,512]{1,0:T(8,128)S(1)}, f32[5,128,128]{2,1,0:T(8,128)S(1)}, f32[5,128,128]{2,1,0:T(8,128)S(1)}) custom-call(s32[2]{0:T(128)S(1)} %pad_add_fusion.scalars, f32[34,128,128]{2,1,0:T(8,128)S(1)} %bitcast.10, f32[34,128,128]{2,1,0:T(8,128)} %copy-done.4, f32[256,1024]{1,0:T(8,128)S(1)} %copy-done.1, f32[256,512]{1,0:T(8,128)S(1)} %copy-done.3), custom_call_target="tpu_custom_call" | custom-call | tf_op jit(solution)/shard_map/residual/pallas_call | solution.py:321
  124.9 0.6 collective-permute-start.2
  125.5 1.3 collective-permute-done.2
  126.8 11.1 %all_to_all.39 = f32[16,5,8,128]{3,2,1,0:T(8,128)S(1)} all-to-all(f32[16,5,8,128]{3,2,1,0:T(8,128)S(1)} %bitcast.14), channel_id=1, replica_groups=mesh['grp'=8,'row_0'=4,'row_1'=4,'row_2'=2] {'row_0','row_1'}, dimensions={0} | all-to-all | bytes 655360 | tf_op jit(solution)/shard_map/all_to_all | solution.py:339
  137.9 10.8 %all_to_all.40 = f32[8,5,8,128]{3,2,1,0:T(8,128)S(1)} all-to-all(f32[8,5,8,128]{3,2,1,0:T(8,128)S(1)} %broadcast_in_dim.10), channel_id=1, replica_groups=mesh['grp'=8,'row_0'=4,'row_1'=4,'row_2'=2] {'grp'}, dimensions={0} | all-to-all | bytes 327680 | tf_op jit(solution)/shard_map/all_to_all | solution.py:339
  148.8 11.5 %all_to_all.41 = f32[16,5,8,128]{3,2,1,0:T(8,128)S(1)} all-to-all(f32[16,5,8,128]{3,2,1,0:T(8,128)S(1)} %broadcast_in_dim.11), channel_id=1, replica_groups=mesh['grp'=8,'row_0'=4,'row_1'=4,'row_2'=2] {'row_0','row_1'}, dimensions={0} | all-to-all | bytes 655360 | tf_op jit(solution)/shard_map/all_to_all | solution.py:339
  160.3 4.0 %collective-permute-start.3 = (f32[5,128,128]{2,1,0:T(8,128)S(1)}, f32[5,128,128]{2,1,0:T(8,128)S(1)}, u32[]{:S(2)}, u32[]{:S(2)}) collective-permute-start(f32[5,128,128]{2,1,0:T(8,128)S(1)} %bitcast.11), channel_id=1, source_target_pairs={{0,1},{1,0},{2,3},{3,2},{4,5},{5,4},{6,7},{7,6},{8,9},{9,8},{10,11... | collective-permute-start | bytes 983048 | tf_op jit(solution)/shard_map/ppermute | solution.py:335
  164.3 1.3 collective-permute-done.3.other_ref
  165.5 13.6 %factor.1 = (f32[256,512]{1,0:T(8,128)}, f32[512,512]{1,0:T(8,128)}) custom-call(s32[2]{0:T(128)S(1)} %pad_add_fusion.scalars, f32[5,128,128]{2,1,0:T(8,128)S(1)} %bitcast.12, f32[5,128,128]{2,1,0:T(8,128)S(1)} %collective-permute-done.3.other_ref, f32[256,512]{1,0:T(8,128)S(1)} %get-tuple-element.11.residual_ref), custom_call_target="tpu_custom_call" | custom-call | tf_op jit(solution)/shard_map/factor/pallas_call | solution.py:321
  (9 shorter events, 0.2 us)
Async XLA Ops:
  1.4 1.2 copy-start
  2.6 1.0 copy-start.2
  8.3 7.3 %collective-permute-start = (f32[34,128,128]{2,1,0:T(8,128)S(1)}, f32[34,128,128]{2,1,0:T(8,128)S(1)}, u32[]{:S(2)}, u32[]{:S(2)}) collective-permute-start(f32[34,128,128]{2,1,0:T(8,128)S(1)} %get-tuple-element.8), channel_id=1, source_target_pairs={{0,1},{1,0},{2,3},{3,2},{4,5},{5,4},{6,7},{7,6},{8,9},{9,8},{10,11... | collective-permute-start | bytes 6684680 | tf_op jit(solution)/shard_map/ppermute | solution.py:335
  77.0 39.4 %copy-start.1 = (f32[256,1024]{1,0:T(8,128)S(1)}, f32[256,1024]{1,0:T(8,128)}, u32[]{:S(2)}) copy-start(f32[256,1024]{1,0:T(8,128)} %basis_ref.3) | copy-start | bytes 3145732
  77.0 39.4 %copy-start.3 = (f32[256,512]{1,0:T(8,128)S(1)}, f32[256,512]{1,0:T(8,128)}, u32[]{:S(2)}) copy-start(f32[256,512]{1,0:T(8,128)} %block_ref.3) | copy-start | bytes 1572868
  105.6 9.4 %collective-permute-start.1 = (f32[34,128,128]{2,1,0:T(8,128)S(1)}, f32[34,128,128]{2,1,0:T(8,128)S(1)}, u32[]{:S(2)}, u32[]{:S(2)}) collective-permute-start(f32[34,128,128]{2,1,0:T(8,128)S(1)} %bitcast.9), channel_id=1, source_target_pairs={{0,1},{1,0},{2,3},{3,2},{4,5},{5,4},{6,7},{7,6},{8,9},{9,8},{10,11... | collective-permute-start | bytes 6684680 | tf_op jit(solution)/shard_map/ppermute | solution.py:335
  115.0 1.4 copy-start.4
  124.9 1.9 %collective-permute-start.2 = (f32[5,128,128]{2,1,0:T(8,128)S(1)}, f32[5,128,128]{2,1,0:T(8,128)S(1)}, u32[]{:S(2)}, u32[]{:S(2)}) collective-permute-start(f32[5,128,128]{2,1,0:T(8,128)S(1)} %get-tuple-element.10), channel_id=1, source_target_pairs={{0,1},{1,0},{2,3},{3,2},{4,5},{5,4},{6,7},{7,6},{8,9},{9,8},{10,11... | collective-permute-start | bytes 983048 | tf_op jit(solution)/shard_map/ppermute | solution.py:335
  160.3 5.2 %collective-permute-start.3 = (f32[5,128,128]{2,1,0:T(8,128)S(1)}, f32[5,128,128]{2,1,0:T(8,128)S(1)}, u32[]{:S(2)}, u32[]{:S(2)}) collective-permute-start(f32[5,128,128]{2,1,0:T(8,128)S(1)} %bitcast.11), channel_id=1, source_target_pairs={{0,1},{1,0},{2,3},{3,2},{4,5},{5,4},{6,7},{7,6},{8,9},{9,8},{10,11... | collective-permute-start | bytes 983048 | tf_op jit(solution)/shard_map/ppermute | solution.py:335

commit v2 on v1

--- a/solution.py
+++ b/solution.py
@@ -9,8 +9,10 @@
 from jax.sharding import PartitionSpec as P
 
 ROW = ("row_0", "row_1", "row_2")
-GRP_ROW = ("grp", "row_0", "row_1", "row_2")
+GRP = ("grp_0", "grp_1")
+GRP_ROW = (*GRP, *ROW)
 PLANE = ("row_0", "row_1")
+SLAB = ("grp_1", "row_0", "row_1")
 
 BLOCK = 128
 STEP = 64
@@ -344,26 +346,18 @@
     return exchange(jnp.broadcast_to(x[None], (count, *x.shape)), axes)
 
 
-def sum_halves(keep, send, spread):
-    total = (keep + swap_cores(send)).reshape(-1, 8, 128)
-    plane = lax.axis_size(PLANE)
-    part = jnp.sum(exchange(total.reshape(plane, -1, 8, 128), PLANE), axis=0)
-    if spread:
-        grp = lax.axis_size("grp")
-        lines = part.shape[0]
-        padded = jnp.pad(part, ((0, -lines % grp), (0, 0), (0, 0)))
-        part = jnp.sum(exchange(padded.reshape(grp, -1, 8, 128), "grp"), axis=0)
-        part = to_all(part, "grp").reshape(-1, 8, 128)[:lines]
-    else:
-        part = jnp.sum(to_all(part, "grp"), axis=0)
-    whole = to_all(part, PLANE).reshape(keep.shape)
+def sum_halves(keep, send, near, far):
+    total = (keep + swap_cores(send)).reshape(lax.axis_size(near), -1, 8, 128)
+    part = jnp.sum(exchange(total, near), axis=0)
+    part = jnp.sum(to_all(part, far), axis=0)
+    whole = to_all(part, near).reshape(keep.shape)
     return whole, swap_cores(whole)
 
 
 def body(basis, block, counts):
     row_slots, size = block.shape
     m, k = basis.shape[1] // BLOCK, size // BLOCK
-    devices = lax.axis_size("grp") * lax.axis_size(ROW)
+    devices = lax.axis_size(GRP) * lax.axis_size(ROW)
     weight = 1.0 / (row_slots * devices)
     scalars = jnp.stack([counts[0, 0], lax.axis_index("row_2").astype(jnp.int32)])
     tiles = (m * (m + 1) // 2 + m * k) // 2
@@ -373,7 +367,7 @@
     keep, send = call(
         functools.partial(products_kernel, weight=weight), [half, half], [], "products"
     )(scalars, basis, block)
-    own, other = sum_halves(keep, send, True)
+    own, other = sum_halves(keep, send, SLAB, "grp_0")
     wide = pltpu.VMEM((m * BLOCK, m * BLOCK), jnp.bfloat16)
     residual, keep, send = call(
         functools.partial(residual_kernel, weight=weight),
@@ -381,7 +375,7 @@
         [wide, wide],
         "residual",
     )(scalars, own, other, basis, block)
-    own, other = sum_halves(keep, send, False)
+    own, other = sum_halves(keep, send, PLANE, GRP)
     new_block, factor = call(
         factor_kernel,
         [block.shape, (size, size)],
@@ -395,9 +389,7 @@
 
 
 def solution(mesh):
-    torus = Mesh(
-        mesh.devices.reshape(mesh.shape["grp"], 4, 4, 2), ("grp", "row_0", "row_1", "row_2")
-    )
-    in_specs = (P(GRP_ROW, None), P(GRP_ROW, None), P("grp", ROW))
+    torus = Mesh(mesh.devices.reshape(mesh.shape["grp"] // 2, 2, 4, 4, 2), GRP_ROW)
+    in_specs = (P(GRP_ROW, None), P(GRP_ROW, None), P(GRP, ROW))
     out_specs = (P(GRP_ROW, None), P())
     return jax.shard_map(body, mesh=torus, in_specs=in_specs, out_specs=out_specs, check_vma=False)

time: 180 us -> 174 us (0.967)
  blocking collectives: 123 us -> 117 us
    all_to_all x7 -> x6, blocking collectives: 123 us -> 117 us  [exchange(): return lax.all_to_all(x, axes, 0, 0, tiled=True)]
where the time goes in v2:
time: 174 us; the launch traced here: 173 us
  blocking collectives  117 us (67%)
  Pallas kernels  26.8 us (15%)
  starting transfers between devices  13.2 us (8%)
  waiting for transfers between devices  10.5 us (6%)
  local copies, waits for them, and re-layouts  3.87 us (2%)
    all_to_all x6, blocking collectives, exchange(): return lax.all_to_all(x, axes, 0, 0, tiled=True)  117 us
    pallas_call x3, Pallas kernels, run(): pl.pallas_call(kernel, out_shape=[jax.ShapeDtypeStruct(s, jnp.float32) fo...  26.8 us
    ppermute x4, starting transfers between devices, swap_cores(): return lax.ppermute(x, 'row_2', [(0, 1), (1, 0)])  13.2 us
    ppermute x4, waiting for transfers between devices, swap_cores(): return lax.ppermute(x, 'row_2', [(0, 1), (1, 0)])  10.5 us
    unnamed x10, local copies, waits for them, and re-layouts  3.67 us
  transfers between devices with their start and end apart: 4, of which 4 were waited for; matrix products, arithmetic and copies ran while one was open for 0% of the time, Pallas kernels for 0%

profile of v2, /device:TPU:1, one launch (start us, length us, event | category | flops | bytes accessed | tf_op | source)
XLA Modules:
  0.0 173.1 jit_solution(4146971053425277831)
XLA Ops:
  1.3 0.1 pad_add_fusion.scalars
  1.4 0.0 copy-start
  1.4 1.2 copy-done
  2.6 0.0 copy-start.2
  2.6 1.0 copy-done.2
  3.6 4.7 %products.1 = (f32[34,128,128]{2,1,0:T(8,128)S(1)}, f32[34,128,128]{2,1,0:T(8,128)S(1)}) custom-call(s32[2]{0:T(128)S(1)} %pad_add_fusion.scalars, f32[256,1024]{1,0:T(8,128)S(1)} %copy-done, f32[256,512]{1,0:T(8,128)S(1)} %copy-done.2), custom_call_target="tpu_custom_call" | custom-call | tf_op jit(solution)/shard_map/products/pallas_call | solution.py:323
  8.3 3.3 %collective-permute-start = (f32[34,128,128]{2,1,0:T(8,128)S(1)}, f32[34,128,128]{2,1,0:T(8,128)S(1)}, u32[]{:S(2)}, u32[]{:S(2)}) collective-permute-start(f32[34,128,128]{2,1,0:T(8,128)S(1)} %get-tuple-element.8), channel_id=1, source_target_pairs={{0,1},{1,0},{2,3},{3,2},{4,5},{5,4},{6,7},{7,6},{8,9},{9,8},{10,11... | collective-permute-start | bytes 6684680 | tf_op jit(solution)/shard_map/ppermute | solution.py:337
  11.7 4.0 %collective-permute-done = f32[34,128,128]{2,1,0:T(8,128)S(1)} collective-permute-done((f32[34,128,128]{2,1,0:T(8,128)S(1)}, f32[34,128,128]{2,1,0:T(8,128)S(1)}, u32[]{:S(2)}, u32[]{:S(2)}) %collective-permute-start) | collective-permute-done | bytes 2228256 | tf_op jit(solution)/shard_map/ppermute | solution.py:337
  15.6 0.4 add.6
  16.0 35.8 %all_to_all.30 = f32[32,17,8,128]{3,2,1,0:T(8,128)S(1)} all-to-all(f32[32,17,8,128]{3,2,1,0:T(8,128)S(1)} %bitcast.11), channel_id=1, replica_groups=mesh['grp_0'=4,'grp_1'=2,'row_0'=4,'row_1'=4,'row_2'=2] {'grp_1','row_0'..., dimensions={0} | all-to-all | bytes 4456448 | tf_op jit(solution)/shard_map/all_to_all | solution.py:341
  51.8 0.1 reduce_sum.36
  51.9 16.4 %all_to_all.31 = f32[4,17,8,128]{3,2,1,0:T(8,128)S(1)} all-to-all(f32[4,17,8,128]{3,2,1,0:T(8,128)S(1)} %broadcast_in_dim.8), channel_id=1, replica_groups=mesh['grp_0'=4,'grp_1'=2,'row_0'=4,'row_1'=4,'row_2'=2] {'grp_0'}, dimensions={0} | all-to-all | bytes 557056 | tf_op jit(solution)/shard_map/all_to_all | solution.py:341
  68.4 0.1 broadcast_in_dim.9
  68.5 0.0 copy-start.1
  68.6 0.0 copy-start.3
  68.6 29.7 %all_to_all.32 = f32[32,17,8,128]{3,2,1,0:T(8,128)S(1)} all-to-all(f32[32,17,8,128]{3,2,1,0:T(8,128)S(1)} %broadcast_in_dim.9), channel_id=1, replica_groups=mesh['grp_0'=4,'grp_1'=2,'row_0'=4,'row_1'=4,'row_2'=2] {'grp_1','row_0'..., dimensions={0} | all-to-all | bytes 4456448 | tf_op jit(solution)/shard_map/all_to_all | solution.py:341
  98.2 4.9 %collective-permute-start.1 = (f32[34,128,128]{2,1,0:T(8,128)S(1)}, f32[34,128,128]{2,1,0:T(8,128)S(1)}, u32[]{:S(2)}, u32[]{:S(2)}) collective-permute-start(f32[34,128,128]{2,1,0:T(8,128)S(1)} %bitcast.7), channel_id=1, source_target_pairs={{0,1},{1,0},{2,3},{3,2},{4,5},{5,4},{6,7},{7,6},{8,9},{9,8},{10,11... | collective-permute-start | bytes 6684680 | tf_op jit(solution)/shard_map/ppermute | solution.py:337
  103.1 4.0 %collective-permute-done.1.other_ref = f32[34,128,128]{2,1,0:T(8,128)S(1)} collective-permute-done((f32[34,128,128]{2,1,0:T(8,128)S(1)}, f32[34,128,128]{2,1,0:T(8,128)S(1)}, u32[]{:S(2)}, u32[]{:S(2)}) %collective-permute-start.1) | collective-permute-done | bytes 2228256 | tf_op jit(solution)/shard_map/ppermute | solution.py:337
  107.1 0.0 copy-start.4
  107.1 1.4 copy-done.4
  108.5 0.0 copy-done.1
  108.5 0.0 copy-done.3
  108.5 8.5 %residual.1 = (f32[256,512]{1,0:T(8,128)S(1)}, f32[5,128,128]{2,1,0:T(8,128)S(1)}, f32[5,128,128]{2,1,0:T(8,128)S(1)}) custom-call(s32[2]{0:T(128)S(1)} %pad_add_fusion.scalars, f32[34,128,128]{2,1,0:T(8,128)S(1)} %bitcast.8, f32[34,128,128]{2,1,0:T(8,128)} %copy-done.4, f32[256,1024]{1,0:T(8,128)S(1)} %copy-done.1, f32[256,512]{1,0:T(8,128)S(1)} %copy-done.3), custom_call_target="tpu_custom_call" | custom-call | tf_op jit(solution)/shard_map/residual/pallas_call | solution.py:323
  117.0 0.6 collective-permute-start.2
  117.7 1.3 collective-permute-done.2
  119.0 11.0 %all_to_all.33 = f32[16,5,8,128]{3,2,1,0:T(8,128)S(1)} all-to-all(f32[16,5,8,128]{3,2,1,0:T(8,128)S(1)} %bitcast.12), channel_id=1, replica_groups=mesh['grp_0'=4,'grp_1'=2,'row_0'=4,'row_1'=4,'row_2'=2] {'row_0','row_1'}, dimensions={0} | all-to-all | bytes 655360 | tf_op jit(solution)/shard_map/all_to_all | solution.py:341
  130.0 12.4 %all_to_all.34 = f32[8,5,8,128]{3,2,1,0:T(8,128)S(1)} all-to-all(f32[8,5,8,128]{3,2,1,0:T(8,128)S(1)} %broadcast_in_dim.10), channel_id=1, replica_groups=mesh['grp_0'=4,'grp_1'=2,'row_0'=4,'row_1'=4,'row_2'=2] {'grp_0','grp_1'}, dimensions={0} | all-to-all | bytes 327680 | tf_op jit(solution)/shard_map/all_to_all | solution.py:341
  142.5 11.5 %all_to_all.35 = f32[16,5,8,128]{3,2,1,0:T(8,128)S(1)} all-to-all(f32[16,5,8,128]{3,2,1,0:T(8,128)S(1)} %broadcast_in_dim.11), channel_id=1, replica_groups=mesh['grp_0'=4,'grp_1'=2,'row_0'=4,'row_1'=4,'row_2'=2] {'row_0','row_1'}, dimensions={0} | all-to-all | bytes 655360 | tf_op jit(solution)/shard_map/all_to_all | solution.py:341
  153.9 4.3 %collective-permute-start.3 = (f32[5,128,128]{2,1,0:T(8,128)S(1)}, f32[5,128,128]{2,1,0:T(8,128)S(1)}, u32[]{:S(2)}, u32[]{:S(2)}) collective-permute-start(f32[5,128,128]{2,1,0:T(8,128)S(1)} %bitcast.9), channel_id=1, source_target_pairs={{0,1},{1,0},{2,3},{3,2},{4,5},{5,4},{6,7},{7,6},{8,9},{9,8},{10,11... | collective-permute-start | bytes 983048 | tf_op jit(solution)/shard_map/ppermute | solution.py:337
  158.3 1.3 collective-permute-done.3.other_ref
  159.5 13.6 %factor.1 = (f32[256,512]{1,0:T(8,128)}, f32[512,512]{1,0:T(8,128)}) custom-call(s32[2]{0:T(128)S(1)} %pad_add_fusion.scalars, f32[5,128,128]{2,1,0:T(8,128)S(1)} %bitcast.10, f32[5,128,128]{2,1,0:T(8,128)S(1)} %collective-permute-done.3.other_ref, f32[256,512]{1,0:T(8,128)S(1)} %get-tuple-element.11.residual_ref), custom_call_target="tpu_custom_call" | custom-call | tf_op jit(solution)/shard_map/factor/pallas_call | solution.py:323
  (7 shorter events, 0.1 us)
Async XLA Ops:
  1.4 1.2 copy-start
  2.6 1.0 copy-start.2
  8.3 7.3 %collective-permute-start = (f32[34,128,128]{2,1,0:T(8,128)S(1)}, f32[34,128,128]{2,1,0:T(8,128)S(1)}, u32[]{:S(2)}, u32[]{:S(2)}) collective-permute-start(f32[34,128,128]{2,1,0:T(8,128)S(1)} %get-tuple-element.8), channel_id=1, source_target_pairs={{0,1},{1,0},{2,3},{3,2},{4,5},{5,4},{6,7},{7,6},{8,9},{9,8},{10,11... | collective-permute-start | bytes 6684680 | tf_op jit(solution)/shard_map/ppermute | solution.py:337
  68.5 40.0 %copy-start.1 = (f32[256,1024]{1,0:T(8,128)S(1)}, f32[256,1024]{1,0:T(8,128)}, u32[]{:S(2)}) copy-start(f32[256,1024]{1,0:T(8,128)} %basis_ref.3) | copy-start | bytes 3145732
  68.6 40.0 %copy-start.3 = (f32[256,512]{1,0:T(8,128)S(1)}, f32[256,512]{1,0:T(8,128)}, u32[]{:S(2)}) copy-start(f32[256,512]{1,0:T(8,128)} %block_ref.3) | copy-start | bytes 1572868
  98.2 8.9 %collective-permute-start.1 = (f32[34,128,128]{2,1,0:T(8,128)S(1)}, f32[34,128,128]{2,1,0:T(8,128)S(1)}, u32[]{:S(2)}, u32[]{:S(2)}) collective-permute-start(f32[34,128,128]{2,1,0:T(8,128)S(1)} %bitcast.7), channel_id=1, source_target_pairs={{0,1},{1,0},{2,3},{3,2},{4,5},{5,4},{6,7},{7,6},{8,9},{9,8},{10,11... | collective-permute-start | bytes 6684680 | tf_op jit(solution)/shard_map/ppermute | solution.py:337
  107.1 1.4 copy-start.4
  117.0 1.9 %collective-permute-start.2 = (f32[5,128,128]{2,1,0:T(8,128)S(1)}, f32[5,128,128]{2,1,0:T(8,128)S(1)}, u32[]{:S(2)}, u32[]{:S(2)}) collective-permute-start(f32[5,128,128]{2,1,0:T(8,128)S(1)} %get-tuple-element.10), channel_id=1, source_target_pairs={{0,1},{1,0},{2,3},{3,2},{4,5},{5,4},{6,7},{7,6},{8,9},{9,8},{10,11... | collective-permute-start | bytes 983048 | tf_op jit(solution)/shard_map/ppermute | solution.py:337
  153.9 5.6 %collective-permute-start.3 = (f32[5,128,128]{2,1,0:T(8,128)S(1)}, f32[5,128,128]{2,1,0:T(8,128)S(1)}, u32[]{:S(2)}, u32[]{:S(2)}) collective-permute-start(f32[5,128,128]{2,1,0:T(8,128)S(1)} %bitcast.9), channel_id=1, source_target_pairs={{0,1},{1,0},{2,3},{3,2},{4,5},{5,4},{6,7},{7,6},{8,9},{9,8},{10,11... | collective-permute-start | bytes 983048 | tf_op jit(solution)/shard_map/ppermute | solution.py:337

commit v3 on v2

--- a/solution.py
+++ b/solution.py
@@ -149,20 +149,17 @@
         send_ref[place] = tile
 
 
-def products_kernel(scalars, basis_ref, block_ref, keep_ref, send_ref, *, weight):
+def overlaps_kernel(scalars, basis_ref, keep_ref, send_ref, *, weight):
     count, core = scalars[0], scalars[1]
     basis = masked(basis_ref, count)
-    block = masked(block_ref, count)
     turned = split(jnp.transpose(basis * weight))
     basis = split(basis)
-    block = split(block)
-    m, k = basis_ref.shape[1] // BLOCK, block_ref.shape[1] // BLOCK
+    m = basis_ref.shape[1] // BLOCK
     half_size = keep_ref.shape[0]
     position = 0
     for i in range(m):
         left = rows_of(turned, i * BLOCK, (i + 1) * BLOCK)
         own = dot3(left, columns_of(basis, i * BLOCK, m * BLOCK))
-        cross = dot3(left, block)
         rest = jnp.dot(
             left[1],
             basis[1][:, i * BLOCK : (i + 1) * BLOCK],
@@ -170,7 +167,6 @@
         )
         tiles = [own[:, j * BLOCK : (j + 1) * BLOCK] for j in range(m - i)]
         tiles[0] = tiles[0] + rest
-        tiles += [cross[:, j * BLOCK : (j + 1) * BLOCK] for j in range(k)]
         for tile in tiles:
             put_by_core(
                 core, keep_ref, send_ref, position // half_size, position % half_size, tile
@@ -178,43 +174,58 @@
             position += 1
 
 
+def products_kernel(scalars, basis_ref, block_ref, keep_ref, send_ref, *, weight):
+    count, core = scalars[0], scalars[1]
+    turned = split(jnp.transpose(masked(basis_ref, count) * weight))
+    block = split(masked(block_ref, count))
+    m, k = basis_ref.shape[1] // BLOCK, block_ref.shape[1] // BLOCK
+    half_size = keep_ref.shape[0]
+    for i in range(m):
+        cross = dot3(rows_of(turned, i * BLOCK, (i + 1) * BLOCK), block)
+        for j in range(k):
+            position = i * k + j
+            put_by_core(
+                core, keep_ref, send_ref, position // half_size, position % half_size,
+                cross[:, j * BLOCK : (j + 1) * BLOCK],
+            )
+
+
+def tile_of(core, own_ref, other_ref, position):
+    half_size = own_ref.shape[0]
+    here = core == position // half_size
+    return jnp.where(here, own_ref[position % half_size], other_ref[position % half_size])
+
+
+def defect_kernel(scalars, own_ref, other_ref, hi_ref, lo_ref):
+    core = scalars[1]
+    m = hi_ref.shape[0] // BLOCK
+    eye = identity(BLOCK)
+    for position, (i, j) in enumerate(upper_pairs(m)):
+        tile = -tile_of(core, own_ref, other_ref, position)
+        if i == j:
+            tile = eye + tile
+        rows, columns = slice(i * BLOCK, (i + 1) * BLOCK), slice(j * BLOCK, (j + 1) * BLOCK)
+        hi_ref[rows, columns], lo_ref[rows, columns] = split(tile)
+        if i != j:
+            hi_ref[columns, rows], lo_ref[columns, rows] = split(jnp.transpose(tile))
+
+
 def residual_kernel(
-    scalars, own_ref, other_ref, basis_ref, block_ref, residual_ref, keep_ref, send_ref,
-    s_hi, s_lo, *, weight
+    scalars, own_ref, other_ref, hi_ref, lo_ref, basis_ref, block_ref,
+    residual_ref, keep_ref, send_ref, *, weight
 ):
     count, core = scalars[0], scalars[1]
     m, k = basis_ref.shape[1] // BLOCK, block_ref.shape[1] // BLOCK
-    half_size = own_ref.shape[0]
-    first = core == 0
-
-    def tile_at(position):
-        mine, theirs = own_ref[position % half_size], other_ref[position % half_size]
-        swap = first if position < half_size else jnp.logical_not(first)
-        return jnp.where(swap, mine, theirs)
-
-    position = 0
-    coeffs = []
-    eye = identity(BLOCK)
-    for i in range(m):
-        for j in range(i, m):
-            tile = -tile_at(position)
-            position += 1
-            if i == j:
-                tile = eye + tile
-            hi, lo = split(tile)
-            s_hi[i * BLOCK : (i + 1) * BLOCK, j * BLOCK : (j + 1) * BLOCK] = hi
-            s_lo[i * BLOCK : (i + 1) * BLOCK, j * BLOCK : (j + 1) * BLOCK] = lo
-            if i != j:
-                hi, lo = split(jnp.transpose(tile))
-                s_hi[j * BLOCK : (j + 1) * BLOCK, i * BLOCK : (i + 1) * BLOCK] = hi
-                s_lo[j * BLOCK : (j + 1) * BLOCK, i * BLOCK : (i + 1) * BLOCK] = lo
-        row = []
-        for j in range(k):
-            row.append(tile_at(position))
-            position += 1
-        coeffs.append(jnp.concatenate(row, axis=1))
-    coeffs = jnp.concatenate(coeffs, axis=0)
-    total = coeffs + dot3((s_hi[...], s_lo[...]), split(coeffs))
+    coeffs = jnp.concatenate(
+        [
+            jnp.concatenate(
+                [tile_of(core, own_ref, other_ref, i * k + j) for j in range(k)], axis=1
+            )
+            for i in range(m)
+        ],
+        axis=0,
+    )
+    total = coeffs + dot3((hi_ref[...], lo_ref[...]), split(coeffs))
     basis = masked(basis_ref, count)
     residual = masked(block_ref, count) - jnp.dot(
         basis, total, precision=HIGHEST, preferred_element_type=jnp.float32
@@ -317,16 +328,16 @@
             )
 
 
-def call(kernel, out_shapes, scratch, name):
+def call(kernel, out_shapes, scratch, name, dtype=jnp.float32):
     def run(scalars, *arrays):
         vmem = pl.BlockSpec(memory_space=pltpu.VMEM)
         return pl.pallas_call(
             kernel,
-            out_shape=[jax.ShapeDtypeStruct(s, jnp.float32) for s in out_shapes],
+            out_shape=[jax.ShapeDtypeStruct(s, dtype) for s in out_shapes],
             in_specs=[pl.BlockSpec(memory_space=pltpu.SMEM)] + [vmem] * len(arrays),
             out_specs=[vmem] * len(out_shapes),
             scratch_shapes=scratch,
-            compiler_params=pltpu.CompilerParams(vmem_limit_bytes=48 << 20),
+            compiler_params=pltpu.CompilerParams(vmem_limit_bytes=24 << 20),
             name=name,
         )(scalars, *arrays)
 
@@ -346,11 +357,22 @@
     return exchange(jnp.broadcast_to(x[None], (count, *x.shape)), axes)
 
 
-def sum_halves(keep, send, near, far):
+def scattered(keep, send, near):
     total = (keep + swap_cores(send)).reshape(lax.axis_size(near), -1, 8, 128)
-    part = jnp.sum(exchange(total, near), axis=0)
-    part = jnp.sum(to_all(part, far), axis=0)
-    whole = to_all(part, near).reshape(keep.shape)
+    return jnp.sum(exchange(total, near), axis=0)
+
+
+def summed_by_pairs(part, axis):
+    count = lax.axis_size(axis)
+    step = 1
+    while step < count:
+        part = part + lax.ppermute(part, axis, [(i, i ^ step) for i in range(count)])
+        step *= 2
+    return part
+
+
+def gathered(part, near, shape):
+    whole = to_all(part, near).reshape(shape)
     return whole, swap_cores(whole)
 
 
@@ -360,29 +382,39 @@
     devices = lax.axis_size(GRP) * lax.axis_size(ROW)
     weight = 1.0 / (row_slots * devices)
     scalars = jnp.stack([counts[0, 0], lax.axis_index("row_2").astype(jnp.int32)])
-    tiles = (m * (m + 1) // 2 + m * k) // 2
-    gram_tiles = k * (k + 1) // 4
-    half = (tiles, BLOCK, BLOCK)
-    gram_half = (gram_tiles, BLOCK, BLOCK)
+    overlap_half = (m * (m + 1) // 4, BLOCK, BLOCK)
+    product_half = (m * k // 2, BLOCK, BLOCK)
+    gram_half = (k * (k + 1) // 4, BLOCK, BLOCK)
+
     keep, send = call(
-        functools.partial(products_kernel, weight=weight), [half, half], [], "products"
+        functools.partial(overlaps_kernel, weight=weight), [overlap_half] * 2, [], "overlaps"
+    )(scalars, basis)
+    overlaps = scattered(keep, send, SLAB)
+    keep, send = call(
+        functools.partial(products_kernel, weight=weight), [product_half] * 2, [], "products"
     )(scalars, basis, block)
-    own, other = sum_halves(keep, send, SLAB, "grp_0")
-    wide = pltpu.VMEM((m * BLOCK, m * BLOCK), jnp.bfloat16)
+    products = scattered(keep, send, SLAB)
+    overlaps = summed_by_pairs(overlaps, "grp_0")
+    own, other = gathered(overlaps, SLAB, overlap_half)
+    products = summed_by_pairs(products, "grp_0")
+    own_product, other_product = gathered(products, SLAB, product_half)
+    hi, lo = call(defect_kernel, [(m * BLOCK, m * BLOCK)] * 2, [], "defect", jnp.bfloat16)(
+        scalars, own, other
+    )
     residual, keep, send = call(
         functools.partial(residual_kernel, weight=weight),
         [block.shape, gram_half, gram_half],
-        [wide, wide],
+        [],
         "residual",
-    )(scalars, own, other, basis, block)
-    own, other = sum_halves(keep, send, PLANE, GRP)
+    )(scalars, own_product, other_product, hi, lo, basis, block)
+
+    part = scattered(keep, send, PLANE)
+    part = jnp.sum(to_all(part, GRP), axis=0)
+    own, other = gathered(part, PLANE, gram_half)
     new_block, factor = call(
         factor_kernel,
         [block.shape, (size, size)],
-        [
-            pltpu.VMEM((size, size), jnp.float32),
-            pltpu.VMEM((size, size), jnp.float32),
-        ],
+        [pltpu.VMEM((size, size), jnp.float32), pltpu.VMEM((size, size), jnp.float32)],
         "factor",
     )(scalars, own, other, residual)
     return new_block, factor

time: 174 us -> 185 us (1.063)
  blocking collectives: 117 us -> 37.6 us
  starting transfers between devices: 13.2 us -> 66.3 us
  waiting for transfers between devices: 10.5 us -> 42.2 us
  other arithmetic: 0.66 us -> 3.87 us
  Pallas kernels: 26.8 us -> 29.4 us
    all_to_all x6 -> x3, blocking collectives: 117 us -> 37.6 us  [exchange(): return lax.all_to_all(x, axes, 0, 0, tiled=True)]
    all_to_all x0 -> x4, starting transfers between devices: none -> 31.4 us  [exchange(): return lax.all_to_all(x, axes, 0, 0, tiled=True)]
    ppermute x0 -> x4, waiting for transfers between devices: none -> 20 us  [summed_by_pairs(): lax.ppermute(part, axis, [(i, i ^ step) for i in range(count)])]
    all_to_all x0 -> x4, waiting for transfers between devices: none -> 14.8 us  [exchange(): return lax.all_to_all(x, axes, 0, 0, tiled=True)]
    ppermute x0 -> x4, starting transfers between devices: none -> 13.8 us  [summed_by_pairs(): lax.ppermute(part, axis, [(i, i ^ step) for i in range(count)])]
    ppermute x4 -> x6, starting transfers between devices: 13.2 us -> 21.2 us  [swap_cores(): return lax.ppermute(x, 'row_2', [(0, 1), (1, 0)])]
    ppermute x4 -> x6, waiting for transfers between devices: 10.5 us -> 7.3 us  [swap_cores(): return lax.ppermute(x, 'row_2', [(0, 1), (1, 0)])]
    pallas_call x3 -> x5, Pallas kernels: 26.8 us -> 29.4 us  [run(): pl.pallas_call(kernel, out_shape=[jax.ShapeDtypeStruct(s, dtype) for s in...]
  transfers between devices with their start and end apart: 4 -> 14, of which waited for: 4 -> 10; matrix products, arithmetic and copies ran while one was open for 0% -> 1% of each run, Pallas kernels for 0% -> 3%
where the time goes in v3:
time: 185 us; the launch traced here: 184 us
  starting transfers between devices  66.3 us (36%)
  waiting for transfers between devices  42.2 us (23%)
  blocking collectives  37.6 us (20%)
  Pallas kernels  29.4 us (16%)
  other arithmetic  3.87 us (2%)
  local copies, waits for them, and re-layouts  3.48 us (2%)
    all_to_all x3, blocking collectives, exchange(): return lax.all_to_all(x, axes, 0, 0, tiled=True)  37.6 us
    all_to_all x4, starting transfers between devices, exchange(): return lax.all_to_all(x, axes, 0, 0, tiled=True)  31.4 us
    pallas_call x5, Pallas kernels, run(): pl.pallas_call(kernel, out_shape=[jax.ShapeDtypeStruct(s, dtype) for s in...  29.4 us
    ppermute x6, starting transfers between devices, swap_cores(): return lax.ppermute(x, 'row_2', [(0, 1), (1, 0)])  21.2 us
    ppermute x4, waiting for transfers between devices, summed_by_pairs(): lax.ppermute(part, axis, [(i, i ^ step) for i in range(count)])  20 us
    all_to_all x4, waiting for transfers between devices, exchange(): return lax.all_to_all(x, axes, 0, 0, tiled=True)  14.8 us
    ppermute x4, starting transfers between devices, summed_by_pairs(): lax.ppermute(part, axis, [(i, i ^ step) for i in range(count)])  13.8 us
    ppermute x6, waiting for transfers between devices, swap_cores(): return lax.ppermute(x, 'row_2', [(0, 1), (1, 0)])  7.3 us
  transfers between devices with their start and end apart: 14, of which 10 were waited for; matrix products, arithmetic and copies ran while one was open for 1% of the time, Pallas kernels for 3%

profile of v3, /device:TPU:1, one launch (start us, length us, event | category | flops | bytes accessed | tf_op | source)
XLA Modules:
  0.0 184.3 jit_solution(8452225802304917468)
XLA Ops:
  1.3 0.1 pad_add_fusion.scalars
  1.4 0.0 copy-start
  1.4 1.2 copy-done
  2.6 3.6 %overlaps.1 = (f32[18,128,128]{2,1,0:T(8,128)S(1)}, f32[18,128,128]{2,1,0:T(8,128)S(1)}) custom-call(s32[2]{0:T(128)S(1)} %pad_add_fusion.scalars, f32[256,1024]{1,0:T(8,128)S(1)} %copy-done), custom_call_target="tpu_custom_call" | custom-call | tf_op jit(solution)/shard_map/overlaps/pallas_call | solution.py:334
  6.2 3.3 %collective-permute-start.4 = (f32[18,128,128]{2,1,0:T(8,128)S(1)}, f32[18,128,128]{2,1,0:T(8,128)S(1)}, u32[]{:S(2)}, u32[]{:S(2)}) collective-permute-start(f32[18,128,128]{2,1,0:T(8,128)S(1)} %get-tuple-element.14), channel_id=1, source_target_pairs={{0,1},{1,0},{2,3},{3,2},{4,5},{5,4},{6,7},{7,6},{8,9},{9,8},{10,11... | collective-permute-start | bytes 3538952 | tf_op jit(solution)/shard_map/ppermute | solution.py:348
  9.5 2.5 %collective-permute-done.4 = f32[18,128,128]{2,1,0:T(8,128)S(1)} collective-permute-done((f32[18,128,128]{2,1,0:T(8,128)S(1)}, f32[18,128,128]{2,1,0:T(8,128)S(1)}, u32[]{:S(2)}, u32[]{:S(2)}) %collective-permute-start.4) | collective-permute-done | bytes 1179680 | tf_op jit(solution)/shard_map/ppermute | solution.py:348
  12.0 1.2 add.24
  13.2 0.0 copy-start.1
  13.2 0.0 copy-start.2
  13.2 6.9 %all-to-all-start.2 = ((f32[32,9,8,128]{3,2,1,0:T(8,128)}), f32[32,9,8,128]{3,2,1,0:T(8,128)}, u32[]{:S(2)}, u32[]{:S(2)}) async-start(f32[32,9,8,128]{3,2,1,0:T(8,128)} %bitcast.4), calls=%async_computation.2 | async-start | bytes 2359296 | tf_op jit(solution)/shard_map/all_to_all | solution.py:352
  20.1 0.0 copy-done.1
  20.1 0.0 copy-done.2
  20.1 3.0 %products.1 = (f32[16,128,128]{2,1,0:T(8,128)S(1)}, f32[16,128,128]{2,1,0:T(8,128)S(1)}) custom-call(s32[2]{0:T(128)S(1)} %pad_add_fusion.scalars, f32[256,1024]{1,0:T(8,128)S(1)} %copy-done.1, f32[256,512]{1,0:T(8,128)S(1)} %copy-done.2), custom_call_target="tpu_custom_call" | custom-call | tf_op jit(solution)/shard_map/products/pallas_call | solution.py:334
  23.2 0.8 collective-permute-start
  23.9 2.3 %collective-permute-done = f32[16,128,128]{2,1,0:T(8,128)S(1)} collective-permute-done((f32[16,128,128]{2,1,0:T(8,128)S(1)}, f32[16,128,128]{2,1,0:T(8,128)S(1)}, u32[]{:S(2)}, u32[]{:S(2)}) %collective-permute-start) | collective-permute-done | bytes 1048608 | tf_op jit(solution)/shard_map/ppermute | solution.py:348
  26.2 1.1 add.21
  27.3 9.2 %all-to-all-done.2 = f32[32,9,8,128]{3,2,1,0:T(8,128)} async-done(((f32[32,9,8,128]{3,2,1,0:T(8,128)}), f32[32,9,8,128]{3,2,1,0:T(8,128)}, u32[]{:S(2)}, u32[]{:S(2)}) %all-to-all-start.2) | async-done | bytes 1179680 | tf_op jit(solution)/shard_map/all_to_all | solution.py:352
  36.5 5.8 %all-to-all-start = ((f32[32,8,8,128]{3,2,1,0:T(8,128)}), f32[32,8,8,128]{3,2,1,0:T(8,128)S(1)}, u32[]{:S(2)}, u32[]{:S(2)}) async-start(f32[32,8,8,128]{3,2,1,0:T(8,128)} %bitcast.2), calls=%async_computation | async-start | bytes 2097152 | tf_op jit(solution)/shard_map/all_to_all | solution.py:352
  42.3 1.3 reduce_sum.37
  43.7 3.1 %collective-permute-start.5 = (f32[9,8,128]{2,1,0:T(8,128)S(1)}, f32[9,8,128]{2,1,0:T(8,128)S(1)}, u32[]{:S(2)}, u32[]{:S(2)}) collective-permute-start(f32[9,8,128]{2,1,0:T(8,128)S(1)} %reduce_sum.37), channel_id=1, source_target_pairs={{0,64},{64,0},{128,192},{192,128},{1,65},{65,1},{129,193},{193,129... | collective-permute-start | bytes 110600 | tf_op jit(solution)/shard_map/ppermute | solution.py:369
  46.7 6.5 %collective-permute-done.5 = f32[9,8,128]{2,1,0:T(8,128)S(1)} collective-permute-done((f32[9,8,128]{2,1,0:T(8,128)S(1)}, f32[9,8,128]{2,1,0:T(8,128)S(1)}, u32[]{:S(2)}, u32[]{:S(2)}) %collective-permute-start.5) | collective-permute-done | bytes 36896 | tf_op jit(solution)/shard_map/ppermute | solution.py:369
  53.2 6.0 %collective-permute-start.6 = (f32[9,8,128]{2,1,0:T(8,128)S(1)}, f32[9,8,128]{2,1,0:T(8,128)S(1)}, u32[]{:S(2)}, u32[]{:S(2)}) collective-permute-start(f32[9,8,128]{2,1,0:T(8,128)S(1)} %add.25), channel_id=1, source_target_pairs={{0,128},{64,192},{128,0},{192,64},{1,129},{65,193},{129,1},{193,65... | collective-permute-start | bytes 110600 | tf_op jit(solution)/shard_map/ppermute | solution.py:369
  59.2 1.8 collective-permute-done.6
  61.0 0.0 all-to-all-done
  61.0 1.1 broadcast_in_dim.9
  62.1 10.0 %all-to-all-start.3 = ((f32[32,9,8,128]{3,2,1,0:T(8,128)}), f32[32,9,8,128]{3,2,1,0:T(8,128)S(1)}, u32[]{:S(2)}, u32[]{:S(2)}) async-start(f32[32,9,8,128]{3,2,1,0:T(8,128)} %broadcast_in_dim.9), calls=%async_computation.3 | async-start | bytes 2359296 | tf_op jit(solution)/shard_map/all_to_all | solution.py:352
  72.1 0.1 reduce_sum.36
  72.2 0.1 collective-permute-start.1
  72.3 9.3 %collective-permute-done.1 = f32[8,8,128]{2,1,0:T(8,128)S(1)} collective-permute-done((f32[8,8,128]{2,1,0:T(8,128)S(1)}, f32[8,8,128]{2,1,0:T(8,128)S(1)}, u32[]{:S(2)}, u32[]{:S(2)}) %collective-permute-start.1) | collective-permute-done | bytes 32800 | tf_op jit(solution)/shard_map/ppermute | solution.py:369
  81.6 4.7 %collective-permute-start.2 = (f32[8,8,128]{2,1,0:T(8,128)S(1)}, f32[8,8,128]{2,1,0:T(8,128)S(1)}, u32[]{:S(2)}, u32[]{:S(2)}) collective-permute-start(f32[8,8,128]{2,1,0:T(8,128)S(1)} %add.22), channel_id=1, source_target_pairs={{0,128},{64,192},{128,0},{192,64},{1,129},{65,193},{129,1},{193,65... | collective-permute-start | bytes 98312 | tf_op jit(solution)/shard_map/ppermute | solution.py:369
  86.3 2.4 %collective-permute-done.2 = f32[8,8,128]{2,1,0:T(8,128)S(1)} collective-permute-done((f32[8,8,128]{2,1,0:T(8,128)S(1)}, f32[8,8,128]{2,1,0:T(8,128)S(1)}, u32[]{:S(2)}, u32[]{:S(2)}) %collective-permute-start.2) | collective-permute-done | bytes 32800 | tf_op jit(solution)/shard_map/ppermute | solution.py:369
  88.7 0.0 all-to-all-done.3
  88.7 1.1 broadcast_in_dim.8
  89.8 8.7 %all-to-all-start.1 = ((f32[32,8,8,128]{3,2,1,0:T(8,128)}), f32[32,8,8,128]{3,2,1,0:T(8,128)S(1)}, u32[]{:S(2)}, u32[]{:S(2)}) async-start(f32[32,8,8,128]{3,2,1,0:T(8,128)} %broadcast_in_dim.8), calls=%async_computation.1 | async-start | bytes 2097152 | tf_op jit(solution)/shard_map/all_to_all | solution.py:352
  98.5 5.5 %collective-permute-start.7 = (f32[18,128,128]{2,1,0:T(8,128)S(1)}, f32[18,128,128]{2,1,0:T(8,128)}, u32[]{:S(2)}, u32[]{:S(2)}) collective-permute-start(f32[18,128,128]{2,1,0:T(8,128)S(1)} %bitcast.9), channel_id=1, source_target_pairs={{0,1},{1,0},{2,3},{3,2},{4,5},{5,4},{6,7},{7,6},{8,9},{9,8},{10,11... | collective-permute-start | bytes 3538952 | tf_op jit(solution)/shard_map/ppermute | solution.py:348
  104.1 5.6 %all-to-all-done.1 = f32[32,8,8,128]{3,2,1,0:T(8,128)S(1)} async-done(((f32[32,8,8,128]{3,2,1,0:T(8,128)}), f32[32,8,8,128]{3,2,1,0:T(8,128)S(1)}, u32[]{:S(2)}, u32[]{:S(2)}) %all-to-all-start.1) | async-done | bytes 1048608 | tf_op jit(solution)/shard_map/all_to_all | solution.py:352
  109.7 0.0 copy-start.3
  109.7 6.8 %collective-permute-start.3 = (f32[16,128,128]{2,1,0:T(8,128)S(1)}, f32[16,128,128]{2,1,0:T(8,128)S(1)}, u32[]{:S(2)}, u32[]{:S(2)}) collective-permute-start(f32[16,128,128]{2,1,0:T(8,128)S(1)} %bitcast.11), channel_id=1, source_target_pairs={{0,1},{1,0},{2,3},{3,2},{4,5},{5,4},{6,7},{7,6},{8,9},{9,8},{10,11... | collective-permute-start | bytes 3145736 | tf_op jit(solution)/shard_map/ppermute | solution.py:348
  116.5 0.0 collective-permute-done.7.other_ref
  116.5 2.3 %defect.1 = (bf16[1024,1024]{1,0:T(8,128)(2,1)S(1)}, bf16[1024,1024]{1,0:T(8,128)(2,1)S(1)}) custom-call(s32[2]{0:T(128)S(1)} %pad_add_fusion.scalars, f32[18,128,128]{2,1,0:T(8,128)S(1)} %bitcast.10, f32[18,128,128]{2,1,0:T(8,128)} %collective-permute-done.7.other_ref), custom_call_target="tpu_custom_call" | custom-call | tf_op jit(solution)/shard_map/defect/pallas_call | solution.py:334
  118.8 0.0 collective-permute-done.3.other_ref
  118.8 0.0 copy-done.3
  118.8 7.0 %residual.1 = (f32[256,512]{1,0:T(8,128)S(1)}, f32[5,128,128]{2,1,0:T(8,128)S(1)}, f32[5,128,128]{2,1,0:T(8,128)S(1)}) custom-call(s32[2]{0:T(128)S(1)} %pad_add_fusion.scalars, f32[16,128,128]{2,1,0:T(8,128)S(1)} %bitcast.12, f32[16,128,128]{2,1,0:T(8,128)S(1)} %collective-permute-done.3.other_ref, bf16[1024,1024]{1,0:T(8,128)(2,1)S(1)} %get-tuple-element.15.hi_ref, ...), custom_call_target="tpu_custom_call" | custom-call | tf_op jit(solution)/shard_map/residual/pallas_call | solution.py:334
  125.7 0.4 collective-permute-start.8
  126.2 1.3 collective-permute-done.8
  127.5 11.3 %all_to_all.35 = f32[16,5,8,128]{3,2,1,0:T(8,128)S(1)} all-to-all(f32[16,5,8,128]{3,2,1,0:T(8,128)S(1)} %bitcast.15), channel_id=1, replica_groups=mesh['grp_0'=4,'grp_1'=2,'row_0'=4,'row_1'=4,'row_2'=2] {'row_0','row_1'}, dimensions={0} | all-to-all | bytes 655360 | tf_op jit(solution)/shard_map/all_to_all | solution.py:352
  138.9 14.8 %all_to_all.36 = f32[8,5,8,128]{3,2,1,0:T(8,128)S(1)} all-to-all(f32[8,5,8,128]{3,2,1,0:T(8,128)S(1)} %broadcast_in_dim.10), channel_id=1, replica_groups=mesh['grp_0'=4,'grp_1'=2,'row_0'=4,'row_1'=4,'row_2'=2] {'grp_0','grp_1'}, dimensions={0} | all-to-all | bytes 327680 | tf_op jit(solution)/shard_map/all_to_all | solution.py:352
  153.7 11.5 %all_to_all.37 = f32[16,5,8,128]{3,2,1,0:T(8,128)S(1)} all-to-all(f32[16,5,8,128]{3,2,1,0:T(8,128)S(1)} %broadcast_in_dim.11), channel_id=1, replica_groups=mesh['grp_0'=4,'grp_1'=2,'row_0'=4,'row_1'=4,'row_2'=2] {'row_0','row_1'}, dimensions={0} | all-to-all | bytes 655360 | tf_op jit(solution)/shard_map/all_to_all | solution.py:352
  165.2 4.3 %collective-permute-start.9 = (f32[5,128,128]{2,1,0:T(8,128)S(1)}, f32[5,128,128]{2,1,0:T(8,128)S(1)}, u32[]{:S(2)}, u32[]{:S(2)}) collective-permute-start(f32[5,128,128]{2,1,0:T(8,128)S(1)} %bitcast.13), channel_id=1, source_target_pairs={{0,1},{1,0},{2,3},{3,2},{4,5},{5,4},{6,7},{7,6},{8,9},{9,8},{10,11... | collective-permute-start | bytes 983048 | tf_op jit(solution)/shard_map/ppermute | solution.py:348
  169.5 1.3 collective-permute-done.9.other_ref
  170.7 13.6 %factor.1 = (f32[256,512]{1,0:T(8,128)}, f32[512,512]{1,0:T(8,128)}) custom-call(s32[2]{0:T(128)S(1)} %pad_add_fusion.scalars, f32[5,128,128]{2,1,0:T(8,128)S(1)} %bitcast.14, f32[5,128,128]{2,1,0:T(8,128)S(1)} %collective-permute-done.9.other_ref, f32[256,512]{1,0:T(8,128)S(1)} %get-tuple-element.19.residual_ref), custom_call_target="tpu_custom_call" | custom-call | tf_op jit(solution)/shard_map/factor/pallas_call | solution.py:334
  (9 shorter events, 0.1 us)
Async XLA Ops:
  1.4 1.2 copy-start
  6.2 5.8 %collective-permute-start.4 = (f32[18,128,128]{2,1,0:T(8,128)S(1)}, f32[18,128,128]{2,1,0:T(8,128)S(1)}, u32[]{:S(2)}, u32[]{:S(2)}) collective-permute-start(f32[18,128,128]{2,1,0:T(8,128)S(1)} %get-tuple-element.14), channel_id=1, source_target_pairs={{0,1},{1,0},{2,3},{3,2},{4,5},{5,4},{6,7},{7,6},{8,9},{9,8},{10,11... | collective-permute-start | bytes 3538952 | tf_op jit(solution)/shard_map/ppermute | solution.py:348
  13.2 6.9 %copy-start.1 = (f32[256,1024]{1,0:T(8,128)S(1)}, f32[256,1024]{1,0:T(8,128)}, u32[]{:S(2)}) copy-start(f32[256,1024]{1,0:T(8,128)} %basis_ref.5) | copy-start | bytes 3145732
  13.2 6.9 %copy-start.2 = (f32[256,512]{1,0:T(8,128)S(1)}, f32[256,512]{1,0:T(8,128)}, u32[]{:S(2)}) copy-start(f32[256,512]{1,0:T(8,128)} %block_ref.3) | copy-start | bytes 1572868
  13.2 23.3 %all-to-all-start.2 = ((f32[32,9,8,128]{3,2,1,0:T(8,128)}), f32[32,9,8,128]{3,2,1,0:T(8,128)}, u32[]{:S(2)}, u32[]{:S(2)}) async-start(f32[32,9,8,128]{3,2,1,0:T(8,128)} %bitcast.4), calls=%async_computation.2 | async-start | bytes 2359296 | tf_op jit(solution)/shard_map/all_to_all | solution.py:352
  23.2 3.0 %collective-permute-start = (f32[16,128,128]{2,1,0:T(8,128)S(1)}, f32[16,128,128]{2,1,0:T(8,128)S(1)}, u32[]{:S(2)}, u32[]{:S(2)}) collective-permute-start(f32[16,128,128]{2,1,0:T(8,128)S(1)} %get-tuple-element.12), channel_id=1, source_target_pairs={{0,1},{1,0},{2,3},{3,2},{4,5},{5,4},{6,7},{7,6},{8,9},{9,8},{10,11... | collective-permute-start | bytes 3145736 | tf_op jit(solution)/shard_map/ppermute | solution.py:348
  36.5 24.5 %all-to-all-start = ((f32[32,8,8,128]{3,2,1,0:T(8,128)}), f32[32,8,8,128]{3,2,1,0:T(8,128)S(1)}, u32[]{:S(2)}, u32[]{:S(2)}) async-start(f32[32,8,8,128]{3,2,1,0:T(8,128)} %bitcast.2), calls=%async_computation | async-start | bytes 2097152 | tf_op jit(solution)/shard_map/all_to_all | solution.py:352
  43.7 9.5 %collective-permute-start.5 = (f32[9,8,128]{2,1,0:T(8,128)S(1)}, f32[9,8,128]{2,1,0:T(8,128)S(1)}, u32[]{:S(2)}, u32[]{:S(2)}) collective-permute-start(f32[9,8,128]{2,1,0:T(8,128)S(1)} %reduce_sum.37), channel_id=1, source_target_pairs={{0,64},{64,0},{128,192},{192,128},{1,65},{65,1},{129,193},{193,129... | collective-permute-start | bytes 110600 | tf_op jit(solution)/shard_map/ppermute | solution.py:369
  53.2 7.8 %collective-permute-start.6 = (f32[9,8,128]{2,1,0:T(8,128)S(1)}, f32[9,8,128]{2,1,0:T(8,128)S(1)}, u32[]{:S(2)}, u32[]{:S(2)}) collective-permute-start(f32[9,8,128]{2,1,0:T(8,128)S(1)} %add.25), channel_id=1, source_target_pairs={{0,128},{64,192},{128,0},{192,64},{1,129},{65,193},{129,1},{193,65... | collective-permute-start | bytes 110600 | tf_op jit(solution)/shard_map/ppermute | solution.py:369
  62.1 26.6 %all-to-all-start.3 = ((f32[32,9,8,128]{3,2,1,0:T(8,128)}), f32[32,9,8,128]{3,2,1,0:T(8,128)S(1)}, u32[]{:S(2)}, u32[]{:S(2)}) async-start(f32[32,9,8,128]{3,2,1,0:T(8,128)} %broadcast_in_dim.9), calls=%async_computation.3 | async-start | bytes 2359296 | tf_op jit(solution)/shard_map/all_to_all | solution.py:352
  72.2 9.5 %collective-permute-start.1 = (f32[8,8,128]{2,1,0:T(8,128)S(1)}, f32[8,8,128]{2,1,0:T(8,128)S(1)}, u32[]{:S(2)}, u32[]{:S(2)}) collective-permute-start(f32[8,8,128]{2,1,0:T(8,128)S(1)} %reduce_sum.36), channel_id=1, source_target_pairs={{0,64},{64,0},{128,192},{192,128},{1,65},{65,1},{129,193},{193,129... | collective-permute-start | bytes 98312 | tf_op jit(solution)/shard_map/ppermute | solution.py:369
  81.6 7.1 %collective-permute-start.2 = (f32[8,8,128]{2,1,0:T(8,128)S(1)}, f32[8,8,128]{2,1,0:T(8,128)S(1)}, u32[]{:S(2)}, u32[]{:S(2)}) collective-permute-start(f32[8,8,128]{2,1,0:T(8,128)S(1)} %add.22), channel_id=1, source_target_pairs={{0,128},{64,192},{128,0},{192,64},{1,129},{65,193},{129,1},{193,65... | collective-permute-start | bytes 98312 | tf_op jit(solution)/shard_map/ppermute | solution.py:369
  89.8 19.8 %all-to-all-start.1 = ((f32[32,8,8,128]{3,2,1,0:T(8,128)}), f32[32,8,8,128]{3,2,1,0:T(8,128)S(1)}, u32[]{:S(2)}, u32[]{:S(2)}) async-start(f32[32,8,8,128]{3,2,1,0:T(8,128)} %broadcast_in_dim.8), calls=%async_computation.1 | async-start | bytes 2097152 | tf_op jit(solution)/shard_map/all_to_all | solution.py:352
  98.5 17.9 %collective-permute-start.7 = (f32[18,128,128]{2,1,0:T(8,128)S(1)}, f32[18,128,128]{2,1,0:T(8,128)}, u32[]{:S(2)}, u32[]{:S(2)}) collective-permute-start(f32[18,128,128]{2,1,0:T(8,128)S(1)} %bitcast.9), channel_id=1, source_target_pairs={{0,1},{1,0},{2,3},{3,2},{4,5},{5,4},{6,7},{7,6},{8,9},{9,8},{10,11... | collective-permute-start | bytes 3538952 | tf_op jit(solution)/shard_map/ppermute | solution.py:348
  109.7 9.1 %copy-start.3 = (f32[256,512]{1,0:T(8,128)S(1)}, f32[256,512]{1,0:T(8,128)}, u32[]{:S(2)}) copy-start(f32[256,512]{1,0:T(8,128)} %block_ref.3) | copy-start | bytes 1572868
  109.7 9.1 %collective-permute-start.3 = (f32[16,128,128]{2,1,0:T(8,128)S(1)}, f32[16,128,128]{2,1,0:T(8,128)S(1)}, u32[]{:S(2)}, u32[]{:S(2)}) collective-permute-start(f32[16,128,128]{2,1,0:T(8,128)S(1)} %bitcast.11), channel_id=1, source_target_pairs={{0,1},{1,0},{2,3},{3,2},{4,5},{5,4},{6,7},{7,6},{8,9},{9,8},{10,11... | collective-permute-start | bytes 3145736 | tf_op jit(solution)/shard_map/ppermute | solution.py:348
  125.7 1.7 collective-permute-start.8
  165.2 5.5 %collective-permute-start.9 = (f32[5,128,128]{2,1,0:T(8,128)S(1)}, f32[5,128,128]{2,1,0:T(8,128)S(1)}, u32[]{:S(2)}, u32[]{:S(2)}) collective-permute-start(f32[5,128,128]{2,1,0:T(8,128)S(1)} %bitcast.13), channel_id=1, source_target_pairs={{0,1},{1,0},{2,3},{3,2},{4,5},{5,4},{6,7},{7,6},{8,9},{9,8},{10,11... | collective-permute-start | bytes 983048 | tf_op jit(solution)/shard_map/ppermute | solution.py:348

commit v4 on v2

--- a/solution.py
+++ b/solution.py
@@ -9,10 +9,9 @@
 from jax.sharding import PartitionSpec as P
 
 ROW = ("row_0", "row_1", "row_2")
-GRP = ("grp_0", "grp_1")
-GRP_ROW = (*GRP, *ROW)
+GRP = "grp"
+GRP_ROW = (GRP, *ROW)
 PLANE = ("row_0", "row_1")
-SLAB = ("grp_1", "row_0", "row_1")
 
 BLOCK = 128
 STEP = 64
@@ -346,6 +345,47 @@
     return exchange(jnp.broadcast_to(x[None], (count, *x.shape)), axes)
 
 
+def crossed_lines():
+    nx, ny = lax.axis_size("row_0"), lax.axis_size("row_1")
+
+    def at(x, y, core):
+        return (x * ny + y) * 2 + core
+
+    first = [[at(x, y, 0) for x in range(nx)] for y in range(ny)]
+    second = [[at(x, y, 1) for y in range(ny)] for x in range(nx)]
+    return first + second
+
+
+def crossed_sheets():
+    nz, nx, ny = lax.axis_size(GRP), lax.axis_size("row_0"), lax.axis_size("row_1")
+
+    def at(z, x, y, core):
+        return ((z * nx + x) * ny + y) * 2 + core
+
+    first = [[at(z, x, y, 0) for z in range(nz) for y in range(ny)] for x in range(nx)]
+    second = [[at(z, x, y, 1) for z in range(nz) for x in range(nx)] for y in range(ny)]
+    return first + second
+
+
+def exchange_in(x, axes, groups):
+    return lax.all_to_all(x, axes, 0, 0, axis_index_groups=groups, tiled=True)
+
+
+def sum_crossed(keep, send):
+    lines, sheets = crossed_lines(), crossed_sheets()
+    total = (keep + swap_cores(send)).reshape(len(lines[0]), -1, 8, 128)
+    part = jnp.sum(exchange_in(total, ROW, lines), axis=0)
+    size, count = part.shape[0], len(sheets[0])
+    part = jnp.pad(part, ((0, -size % count), (0, 0), (0, 0)))
+    part = part.reshape(count, -1, 8, 128)
+    part = jnp.sum(exchange_in(part, GRP_ROW, sheets), axis=0)
+    part = exchange_in(jnp.broadcast_to(part[None], (count, *part.shape)), GRP_ROW, sheets)
+    part = part.reshape(-1, 8, 128)[:size]
+    whole = jnp.broadcast_to(part[None], (len(lines[0]), *part.shape))
+    whole = exchange_in(whole, ROW, lines).reshape(keep.shape)
+    return whole, swap_cores(whole)
+
+
 def sum_halves(keep, send, near, far):
     total = (keep + swap_cores(send)).reshape(lax.axis_size(near), -1, 8, 128)
     part = jnp.sum(exchange(total, near), axis=0)
@@ -367,7 +407,7 @@
     keep, send = call(
         functools.partial(products_kernel, weight=weight), [half, half], [], "products"
     )(scalars, basis, block)
-    own, other = sum_halves(keep, send, SLAB, "grp_0")
+    own, other = sum_crossed(keep, send)
     wide = pltpu.VMEM((m * BLOCK, m * BLOCK), jnp.bfloat16)
     residual, keep, send = call(
         functools.partial(residual_kernel, weight=weight),
@@ -389,7 +429,7 @@
 
 
 def solution(mesh):
-    torus = Mesh(mesh.devices.reshape(mesh.shape["grp"] // 2, 2, 4, 4, 2), GRP_ROW)
+    torus = Mesh(mesh.devices.reshape(mesh.shape["grp"], 4, 4, 2), GRP_ROW)
     in_specs = (P(GRP_ROW, None), P(GRP_ROW, None), P(GRP, ROW))
     out_specs = (P(GRP_ROW, None), P())
     return jax.shard_map(body, mesh=torus, in_specs=in_specs, out_specs=out_specs, check_vma=False)

time: 174 us -> 181 us (1.040)
  blocking collectives: 117 us -> 125 us
    all_to_all x0 -> x4, blocking collectives: none -> 91.6 us  [exchange_in(): return lax.all_to_all(x, axes, 0, 0, axis_index_groups=groups, tiled=True)]
    all_to_all x6 -> x3, blocking collectives: 117 us -> 33.2 us  [exchange(): return lax.all_to_all(x, axes, 0, 0, tiled=True)]
where the time goes in v4:
time: 181 us
  blocking collectives  125 us (69%)
  Pallas kernels  27 us (15%)
  starting transfers between devices  12.2 us (7%)
  waiting for transfers between devices  10.5 us (6%)
  local copies, waits for them, and re-layouts  3.97 us (2%)
    all_to_all x4, blocking collectives, exchange_in(): return lax.all_to_all(x, axes, 0, 0, axis_index_groups=groups, tiled=True)  91.6 us
    all_to_all x3, blocking collectives, exchange(): return lax.all_to_all(x, axes, 0, 0, tiled=True)  33.2 us
    pallas_call x3, Pallas kernels, run(): pl.pallas_call(kernel, out_shape=[jax.ShapeDtypeStruct(s, jnp.float32) fo...  27 us
    ppermute x4, starting transfers between devices, swap_cores(): return lax.ppermute(x, 'row_2', [(0, 1), (1, 0)])  12.2 us
    ppermute x4, waiting for transfers between devices, swap_cores(): return lax.ppermute(x, 'row_2', [(0, 1), (1, 0)])  10.5 us
    unnamed x10, local copies, waits for them, and re-layouts  3.67 us
  transfers between devices with their start and end apart: 4, of which 4 were waited for; matrix products, arithmetic and copies ran while one was open for 0% of the time, Pallas kernels for 0%

profile of v4, /device:TPU:1, one launch (start us, length us, event | category | flops | bytes accessed | tf_op | source)
XLA Modules:
  0.0 180.5 jit_solution(4640460687605023052)
XLA Ops:
  1.3 0.1 pad_add_fusion.scalars
  1.4 0.0 copy-start
  1.4 1.2 copy-done
  2.6 0.0 copy-start.2
  2.6 1.0 copy-done.2
  3.6 4.7 %products.1 = (f32[34,128,128]{2,1,0:T(8,128)S(1)}, f32[34,128,128]{2,1,0:T(8,128)S(1)}) custom-call(s32[2]{0:T(128)S(1)} %pad_add_fusion.scalars, f32[256,1024]{1,0:T(8,128)S(1)} %copy-done, f32[256,512]{1,0:T(8,128)S(1)} %copy-done.2), custom_call_target="tpu_custom_call" | custom-call | tf_op jit(solution)/shard_map/products/pallas_call | solution.py:322
  8.3 3.3 %collective-permute-start = (f32[34,128,128]{2,1,0:T(8,128)S(1)}, f32[34,128,128]{2,1,0:T(8,128)S(1)}, u32[]{:S(2)}, u32[]{:S(2)}) collective-permute-start(f32[34,128,128]{2,1,0:T(8,128)S(1)} %get-tuple-element.8), channel_id=1, source_target_pairs={{0,1},{1,0},{2,3},{3,2},{4,5},{5,4},{6,7},{7,6},{8,9},{9,8},{10,11... | collective-permute-start | bytes 6684680 | tf_op jit(solution)/shard_map/ppermute | solution.py:336
  11.7 4.0 %collective-permute-done = f32[34,128,128]{2,1,0:T(8,128)S(1)} collective-permute-done((f32[34,128,128]{2,1,0:T(8,128)S(1)}, f32[34,128,128]{2,1,0:T(8,128)S(1)}, u32[]{:S(2)}, u32[]{:S(2)}) %collective-permute-start) | collective-permute-done | bytes 2228256 | tf_op jit(solution)/shard_map/ppermute | solution.py:336
  15.6 0.4 add.8
  16.0 18.8 %all_to_all.35 = f32[4,136,8,128]{3,2,1,0:T(8,128)S(1)} all-to-all(f32[4,136,8,128]{3,2,1,0:T(8,128)S(1)} %bitcast.13), channel_id=1, replica_groups={{0,8,16,24},{2,10,18,26},{4,12,20,28},{6,14,22,30},{1,3,5,7},{9,11,13,1..., dimensions={0} | all-to-all | bytes 4456448 | tf_op jit(solution)/shard_map/all_to_all | solution.py:371
  34.8 0.2 reduce_sum.36
  35.1 28.9 %all_to_all.36 = f32[32,5,8,128]{3,2,1,0:T(8,128)S(1)} all-to-all(f32[32,5,8,128]{3,2,1,0:T(8,128)S(1)} %bitcast.14), channel_id=1, replica_groups={{0,2,4,6,32,34,36,38,64,66,68,70,96,98,100,102,128,130,132,134,160,162,..., dimensions={0} | all-to-all | bytes 1310720 | tf_op jit(solution)/shard_map/all_to_all | solution.py:371
  64.0 0.1 reduce_sum.37
  64.1 24.9 %all_to_all.37 = f32[32,5,8,128]{3,2,1,0:T(8,128)S(1)} all-to-all(f32[32,5,8,128]{3,2,1,0:T(8,128)S(1)} %broadcast_in_dim.8), channel_id=1, replica_groups={{0,2,4,6,32,34,36,38,64,66,68,70,96,98,100,102,128,130,132,134,160,162,..., dimensions={0} | all-to-all | bytes 1310720 | tf_op jit(solution)/shard_map/all_to_all | solution.py:371
  89.0 0.1 broadcast_in_dim.9
  89.2 0.0 copy-start.1
  89.2 0.0 copy-start.3
  89.2 19.0 %all_to_all.38 = f32[4,136,8,128]{3,2,1,0:T(8,128)S(1)} all-to-all(f32[4,136,8,128]{3,2,1,0:T(8,128)S(1)} %broadcast_in_dim.9), channel_id=1, replica_groups={{0,8,16,24},{2,10,18,26},{4,12,20,28},{6,14,22,30},{1,3,5,7},{9,11,13,1..., dimensions={0} | all-to-all | bytes 4456448 | tf_op jit(solution)/shard_map/all_to_all | solution.py:371
  108.2 4.1 %collective-permute-start.1 = (f32[34,128,128]{2,1,0:T(8,128)S(1)}, f32[34,128,128]{2,1,0:T(8,128)S(1)}, u32[]{:S(2)}, u32[]{:S(2)}) collective-permute-start(f32[34,128,128]{2,1,0:T(8,128)S(1)} %bitcast.9), channel_id=1, source_target_pairs={{0,1},{1,0},{2,3},{3,2},{4,5},{5,4},{6,7},{7,6},{8,9},{9,8},{10,11... | collective-permute-start | bytes 6684680 | tf_op jit(solution)/shard_map/ppermute | solution.py:336
  112.3 4.0 %collective-permute-done.1.other_ref = f32[34,128,128]{2,1,0:T(8,128)S(1)} collective-permute-done((f32[34,128,128]{2,1,0:T(8,128)S(1)}, f32[34,128,128]{2,1,0:T(8,128)S(1)}, u32[]{:S(2)}, u32[]{:S(2)}) %collective-permute-start.1) | collective-permute-done | bytes 2228256 | tf_op jit(solution)/shard_map/ppermute | solution.py:336
  116.2 0.0 copy-start.4
  116.2 1.4 copy-done.4
  117.6 0.0 copy-done.1
  117.6 0.0 copy-done.3
  117.6 8.7 %residual.1 = (f32[256,512]{1,0:T(8,128)S(1)}, f32[5,128,128]{2,1,0:T(8,128)S(1)}, f32[5,128,128]{2,1,0:T(8,128)S(1)}) custom-call(s32[2]{0:T(128)S(1)} %pad_add_fusion.scalars, f32[34,128,128]{2,1,0:T(8,128)S(1)} %bitcast.10, f32[34,128,128]{2,1,0:T(8,128)} %copy-done.4, f32[256,1024]{1,0:T(8,128)S(1)} %copy-done.1, f32[256,512]{1,0:T(8,128)S(1)} %copy-done.3), custom_call_target="tpu_custom_call" | custom-call | tf_op jit(solution)/shard_map/residual/pallas_call | solution.py:322
  126.3 0.5 collective-permute-start.2
  126.8 1.3 collective-permute-done.2
  128.1 11.2 %all_to_all.39 = f32[16,5,8,128]{3,2,1,0:T(8,128)S(1)} all-to-all(f32[16,5,8,128]{3,2,1,0:T(8,128)S(1)} %bitcast.16), channel_id=1, replica_groups=mesh['grp'=8,'row_0'=4,'row_1'=4,'row_2'=2] {'row_0','row_1'}, dimensions={0} | all-to-all | bytes 655360 | tf_op jit(solution)/shard_map/all_to_all | solution.py:340
  139.4 10.8 %all_to_all.40 = f32[8,5,8,128]{3,2,1,0:T(8,128)S(1)} all-to-all(f32[8,5,8,128]{3,2,1,0:T(8,128)S(1)} %broadcast_in_dim.10), channel_id=1, replica_groups=mesh['grp'=8,'row_0'=4,'row_1'=4,'row_2'=2] {'grp'}, dimensions={0} | all-to-all | bytes 327680 | tf_op jit(solution)/shard_map/all_to_all | solution.py:340
  150.2 11.2 %all_to_all.41 = f32[16,5,8,128]{3,2,1,0:T(8,128)S(1)} all-to-all(f32[16,5,8,128]{3,2,1,0:T(8,128)S(1)} %broadcast_in_dim.11), channel_id=1, replica_groups=mesh['grp'=8,'row_0'=4,'row_1'=4,'row_2'=2] {'row_0','row_1'}, dimensions={0} | all-to-all | bytes 655360 | tf_op jit(solution)/shard_map/all_to_all | solution.py:340
  161.4 4.3 %collective-permute-start.3 = (f32[5,128,128]{2,1,0:T(8,128)S(1)}, f32[5,128,128]{2,1,0:T(8,128)S(1)}, u32[]{:S(2)}, u32[]{:S(2)}) collective-permute-start(f32[5,128,128]{2,1,0:T(8,128)S(1)} %bitcast.11), channel_id=1, source_target_pairs={{0,1},{1,0},{2,3},{3,2},{4,5},{5,4},{6,7},{7,6},{8,9},{9,8},{10,11... | collective-permute-start | bytes 983048 | tf_op jit(solution)/shard_map/ppermute | solution.py:336
  165.7 1.3 collective-permute-done.3.other_ref
  167.0 13.6 %factor.1 = (f32[256,512]{1,0:T(8,128)}, f32[512,512]{1,0:T(8,128)}) custom-call(s32[2]{0:T(128)S(1)} %pad_add_fusion.scalars, f32[5,128,128]{2,1,0:T(8,128)S(1)} %bitcast.12, f32[5,128,128]{2,1,0:T(8,128)S(1)} %collective-permute-done.3.other_ref, f32[256,512]{1,0:T(8,128)S(1)} %get-tuple-element.11.residual_ref), custom_call_target="tpu_custom_call" | custom-call | tf_op jit(solution)/shard_map/factor/pallas_call | solution.py:322
  (8 shorter events, 0.2 us)
Async XLA Ops:
  1.4 1.2 copy-start
  2.6 1.0 copy-start.2
  8.3 7.3 %collective-permute-start = (f32[34,128,128]{2,1,0:T(8,128)S(1)}, f32[34,128,128]{2,1,0:T(8,128)S(1)}, u32[]{:S(2)}, u32[]{:S(2)}) collective-permute-start(f32[34,128,128]{2,1,0:T(8,128)S(1)} %get-tuple-element.8), channel_id=1, source_target_pairs={{0,1},{1,0},{2,3},{3,2},{4,5},{5,4},{6,7},{7,6},{8,9},{9,8},{10,11... | collective-permute-start | bytes 6684680 | tf_op jit(solution)/shard_map/ppermute | solution.py:336
  89.2 28.4 %copy-start.1 = (f32[256,1024]{1,0:T(8,128)S(1)}, f32[256,1024]{1,0:T(8,128)}, u32[]{:S(2)}) copy-start(f32[256,1024]{1,0:T(8,128)} %basis_ref.3) | copy-start | bytes 3145732
  89.2 28.4 %copy-start.3 = (f32[256,512]{1,0:T(8,128)S(1)}, f32[256,512]{1,0:T(8,128)}, u32[]{:S(2)}) copy-start(f32[256,512]{1,0:T(8,128)} %block_ref.3) | copy-start | bytes 1572868
  108.2 8.1 %collective-permute-start.1 = (f32[34,128,128]{2,1,0:T(8,128)S(1)}, f32[34,128,128]{2,1,0:T(8,128)S(1)}, u32[]{:S(2)}, u32[]{:S(2)}) collective-permute-start(f32[34,128,128]{2,1,0:T(8,128)S(1)} %bitcast.9), channel_id=1, source_target_pairs={{0,1},{1,0},{2,3},{3,2},{4,5},{5,4},{6,7},{7,6},{8,9},{9,8},{10,11... | collective-permute-start | bytes 6684680 | tf_op jit(solution)/shard_map/ppermute | solution.py:336
  116.2 1.4 copy-start.4
  126.3 1.7 collective-permute-start.2
  161.4 5.6 %collective-permute-start.3 = (f32[5,128,128]{2,1,0:T(8,128)S(1)}, f32[5,128,128]{2,1,0:T(8,128)S(1)}, u32[]{:S(2)}, u32[]{:S(2)}) collective-permute-start(f32[5,128,128]{2,1,0:T(8,128)S(1)} %bitcast.11), channel_id=1, source_target_pairs={{0,1},{1,0},{2,3},{3,2},{4,5},{5,4},{6,7},{7,6},{8,9},{9,8},{10,11... | collective-permute-start | bytes 983048 | tf_op jit(solution)/shard_map/ppermute | solution.py:336

commit v5 on v2

--- a/solution.py
+++ b/solution.py
@@ -139,17 +139,7 @@
     return jnp.where(rows < count, ref[...], 0.0)
 
 
-def put_by_core(core, keep_ref, send_ref, half, place, tile):
-    @pl.when(core == half)
-    def _():
-        keep_ref[place] = tile
-
-    @pl.when(core != half)
-    def _():
-        send_ref[place] = tile
-
-
-def products_kernel(scalars, basis_ref, block_ref, keep_ref, send_ref, *, weight):
+def products_kernel(scalars, basis_ref, block_ref, keep_ref, send_ref, all_ref, *, weight):
     count, core = scalars[0], scalars[1]
     basis = masked(basis_ref, count)
     block = masked(block_ref, count)
@@ -172,15 +162,15 @@
         tiles[0] = tiles[0] + rest
         tiles += [cross[:, j * BLOCK : (j + 1) * BLOCK] for j in range(k)]
         for tile in tiles:
-            put_by_core(
-                core, keep_ref, send_ref, position // half_size, position % half_size, tile
-            )
+            all_ref[position] = tile
             position += 1
+    keep_ref[...] = all_ref[pl.ds(core * half_size, half_size)]
+    send_ref[...] = all_ref[pl.ds((1 - core) * half_size, half_size)]
 
 
 def residual_kernel(
     scalars, own_ref, other_ref, basis_ref, block_ref, residual_ref, keep_ref, send_ref,
-    s_hi, s_lo, *, weight
+    s_hi, s_lo, gram_ref, *, weight
 ):
     count, core = scalars[0], scalars[1]
     m, k = basis_ref.shape[1] // BLOCK, block_ref.shape[1] // BLOCK
@@ -229,11 +219,10 @@
             rows_of(turned, i * BLOCK, (i + 1) * BLOCK), columns_of(residual, i * BLOCK, k * BLOCK)
         )
         for j in range(k - i):
-            put_by_core(
-                core, keep_ref, send_ref, position // half_size, position % half_size,
-                row[:, j * BLOCK : (j + 1) * BLOCK],
-            )
+            gram_ref[position] = row[:, j * BLOCK : (j + 1) * BLOCK]
             position += 1
+    keep_ref[...] = gram_ref[pl.ds(core * half_size, half_size)]
+    send_ref[...] = gram_ref[pl.ds((1 - core) * half_size, half_size)]
 
 
 def dot3_nt(a, b):
@@ -326,7 +315,7 @@
             in_specs=[pl.BlockSpec(memory_space=pltpu.SMEM)] + [vmem] * len(arrays),
             out_specs=[vmem] * len(out_shapes),
             scratch_shapes=scratch,
-            compiler_params=pltpu.CompilerParams(vmem_limit_bytes=48 << 20),
+            compiler_params=pltpu.CompilerParams(vmem_limit_bytes=24 << 20),
             name=name,
         )(scalars, *arrays)
 
@@ -365,14 +354,15 @@
     half = (tiles, BLOCK, BLOCK)
     gram_half = (gram_tiles, BLOCK, BLOCK)
     keep, send = call(
-        functools.partial(products_kernel, weight=weight), [half, half], [], "products"
+        functools.partial(products_kernel, weight=weight), [half, half],
+        [pltpu.VMEM((2 * tiles, BLOCK, BLOCK), jnp.float32)], "products"
     )(scalars, basis, block)
     own, other = sum_halves(keep, send, SLAB, "grp_0")
     wide = pltpu.VMEM((m * BLOCK, m * BLOCK), jnp.bfloat16)
     residual, keep, send = call(
         functools.partial(residual_kernel, weight=weight),
         [block.shape, gram_half, gram_half],
-        [wide, wide],
+        [wide, wide, pltpu.VMEM((2 * gram_tiles, BLOCK, BLOCK), jnp.float32)],
         "residual",
     )(scalars, own, other, basis, block)
     own, other = sum_halves(keep, send, PLANE, GRP)

time: 174 us -> 168 us (0.966)
  Pallas kernels: 26.8 us -> 23.4 us
    pallas_call x3, Pallas kernels: 26.8 us -> 23.4 us  [run(): pl.pallas_call(kernel, out_shape=[jax.ShapeDtypeStruct(s, jnp.float32) fo...]
    unnamed x10 -> x8, local copies, waits for them, and re-layouts: 3.67 us -> 2.28 us
where the time goes in v5:
time: 168 us
  blocking collectives  117 us (70%)
  Pallas kernels  23.4 us (14%)
  starting transfers between devices  13 us (8%)
  waiting for transfers between devices  10.5 us (6%)
  local copies, waits for them, and re-layouts  2.48 us (1%)
    all_to_all x6, blocking collectives, exchange(): return lax.all_to_all(x, axes, 0, 0, tiled=True)  117 us
    pallas_call x3, Pallas kernels, run(): pl.pallas_call(kernel, out_shape=[jax.ShapeDtypeStruct(s, jnp.float32) fo...  23.4 us
    ppermute x4, starting transfers between devices, swap_cores(): return lax.ppermute(x, 'row_2', [(0, 1), (1, 0)])  13 us
    ppermute x4, waiting for transfers between devices, swap_cores(): return lax.ppermute(x, 'row_2', [(0, 1), (1, 0)])  10.5 us
  transfers between devices with their start and end apart: 4, of which 4 were waited for; matrix products, arithmetic and copies ran while one was open for 0% of the time, Pallas kernels for 0%

profile of v5, /device:TPU:1, one launch (start us, length us, event | category | flops | bytes accessed | tf_op | source)
XLA Modules:
  0.0 168.1 jit_solution(380229418175783078)
XLA Ops:
  1.3 0.1 pad_add_fusion.scalars
  1.4 0.0 copy-start
  1.4 1.2 copy-done
  2.6 0.0 copy-start.2
  2.6 1.0 copy-done.2
  3.6 3.1 %products.1 = (f32[34,128,128]{2,1,0:T(8,128)S(1)}, f32[34,128,128]{2,1,0:T(8,128)S(1)}) custom-call(s32[2]{0:T(128)S(1)} %pad_add_fusion.scalars, f32[256,1024]{1,0:T(8,128)S(1)} %copy-done, f32[256,512]{1,0:T(8,128)S(1)} %copy-done.2), custom_call_target="tpu_custom_call" | custom-call | tf_op jit(solution)/shard_map/products/pallas_call | solution.py:312
  6.8 3.3 %collective-permute-start = (f32[34,128,128]{2,1,0:T(8,128)S(1)}, f32[34,128,128]{2,1,0:T(8,128)S(1)}, u32[]{:S(2)}, u32[]{:S(2)}) collective-permute-start(f32[34,128,128]{2,1,0:T(8,128)S(1)} %get-tuple-element.8), channel_id=1, source_target_pairs={{0,1},{1,0},{2,3},{3,2},{4,5},{5,4},{6,7},{7,6},{8,9},{9,8},{10,11... | collective-permute-start | bytes 6684680 | tf_op jit(solution)/shard_map/ppermute | solution.py:326
  10.1 4.0 %collective-permute-done = f32[34,128,128]{2,1,0:T(8,128)S(1)} collective-permute-done((f32[34,128,128]{2,1,0:T(8,128)S(1)}, f32[34,128,128]{2,1,0:T(8,128)S(1)}, u32[]{:S(2)}, u32[]{:S(2)}) %collective-permute-start) | collective-permute-done | bytes 2228256 | tf_op jit(solution)/shard_map/ppermute | solution.py:326
  14.1 0.3 add.6
  14.3 35.8 %all_to_all.30 = f32[32,17,8,128]{3,2,1,0:T(8,128)S(1)} all-to-all(f32[32,17,8,128]{3,2,1,0:T(8,128)S(1)} %bitcast.11), channel_id=1, replica_groups=mesh['grp_0'=4,'grp_1'=2,'row_0'=4,'row_1'=4,'row_2'=2] {'grp_1','row_0'..., dimensions={0} | all-to-all | bytes 4456448 | tf_op jit(solution)/shard_map/all_to_all | solution.py:330
  50.1 0.1 reduce_sum.36
  50.3 16.4 %all_to_all.31 = f32[4,17,8,128]{3,2,1,0:T(8,128)S(1)} all-to-all(f32[4,17,8,128]{3,2,1,0:T(8,128)S(1)} %broadcast_in_dim.8), channel_id=1, replica_groups=mesh['grp_0'=4,'grp_1'=2,'row_0'=4,'row_1'=4,'row_2'=2] {'grp_0'}, dimensions={0} | all-to-all | bytes 557056 | tf_op jit(solution)/shard_map/all_to_all | solution.py:330
  66.7 0.1 broadcast_in_dim.9
  66.9 0.0 copy-start.1
  66.9 0.0 copy-start.3
  66.9 29.7 %all_to_all.32 = f32[32,17,8,128]{3,2,1,0:T(8,128)S(1)} all-to-all(f32[32,17,8,128]{3,2,1,0:T(8,128)S(1)} %broadcast_in_dim.9), channel_id=1, replica_groups=mesh['grp_0'=4,'grp_1'=2,'row_0'=4,'row_1'=4,'row_2'=2] {'grp_1','row_0'..., dimensions={0} | all-to-all | bytes 4456448 | tf_op jit(solution)/shard_map/all_to_all | solution.py:330
  96.6 4.9 %collective-permute-start.1 = (f32[34,128,128]{2,1,0:T(8,128)S(1)}, f32[34,128,128]{2,1,0:T(8,128)S(1)}, u32[]{:S(2)}, u32[]{:S(2)}) collective-permute-start(f32[34,128,128]{2,1,0:T(8,128)S(1)} %bitcast.7), channel_id=1, source_target_pairs={{0,1},{1,0},{2,3},{3,2},{4,5},{5,4},{6,7},{7,6},{8,9},{9,8},{10,11... | collective-permute-start | bytes 6684680 | tf_op jit(solution)/shard_map/ppermute | solution.py:326
  101.5 4.0 %collective-permute-done.1.other_ref = f32[34,128,128]{2,1,0:T(8,128)S(1)} collective-permute-done((f32[34,128,128]{2,1,0:T(8,128)S(1)}, f32[34,128,128]{2,1,0:T(8,128)S(1)}, u32[]{:S(2)}, u32[]{:S(2)}) %collective-permute-start.1) | collective-permute-done | bytes 2228256 | tf_op jit(solution)/shard_map/ppermute | solution.py:326
  105.5 0.0 copy-done.1
  105.5 0.0 copy-done.3
  105.5 6.7 %residual.1 = (f32[256,512]{1,0:T(8,128)S(1)}, f32[5,128,128]{2,1,0:T(8,128)S(1)}, f32[5,128,128]{2,1,0:T(8,128)S(1)}) custom-call(s32[2]{0:T(128)S(1)} %pad_add_fusion.scalars, f32[34,128,128]{2,1,0:T(8,128)S(1)} %bitcast.8, f32[34,128,128]{2,1,0:T(8,128)S(1)} %collective-permute-done.1.other_ref, f32[256,1024]{1,0:T(8,128)S(1)} %copy-done.1, ...), custom_call_target="tpu_custom_call" | custom-call | tf_op jit(solution)/shard_map/residual/pallas_call | solution.py:312
  112.2 0.5 collective-permute-start.2
  112.7 1.3 collective-permute-done.2
  114.0 11.0 %all_to_all.33 = f32[16,5,8,128]{3,2,1,0:T(8,128)S(1)} all-to-all(f32[16,5,8,128]{3,2,1,0:T(8,128)S(1)} %bitcast.12), channel_id=1, replica_groups=mesh['grp_0'=4,'grp_1'=2,'row_0'=4,'row_1'=4,'row_2'=2] {'row_0','row_1'}, dimensions={0} | all-to-all | bytes 655360 | tf_op jit(solution)/shard_map/all_to_all | solution.py:330
  125.0 12.4 %all_to_all.34 = f32[8,5,8,128]{3,2,1,0:T(8,128)S(1)} all-to-all(f32[8,5,8,128]{3,2,1,0:T(8,128)S(1)} %broadcast_in_dim.10), channel_id=1, replica_groups=mesh['grp_0'=4,'grp_1'=2,'row_0'=4,'row_1'=4,'row_2'=2] {'grp_0','grp_1'}, dimensions={0} | all-to-all | bytes 327680 | tf_op jit(solution)/shard_map/all_to_all | solution.py:330
  137.4 11.5 %all_to_all.35 = f32[16,5,8,128]{3,2,1,0:T(8,128)S(1)} all-to-all(f32[16,5,8,128]{3,2,1,0:T(8,128)S(1)} %broadcast_in_dim.11), channel_id=1, replica_groups=mesh['grp_0'=4,'grp_1'=2,'row_0'=4,'row_1'=4,'row_2'=2] {'row_0','row_1'}, dimensions={0} | all-to-all | bytes 655360 | tf_op jit(solution)/shard_map/all_to_all | solution.py:330
  148.9 4.3 %collective-permute-start.3 = (f32[5,128,128]{2,1,0:T(8,128)S(1)}, f32[5,128,128]{2,1,0:T(8,128)S(1)}, u32[]{:S(2)}, u32[]{:S(2)}) collective-permute-start(f32[5,128,128]{2,1,0:T(8,128)S(1)} %bitcast.9), channel_id=1, source_target_pairs={{0,1},{1,0},{2,3},{3,2},{4,5},{5,4},{6,7},{7,6},{8,9},{9,8},{10,11... | collective-permute-start | bytes 983048 | tf_op jit(solution)/shard_map/ppermute | solution.py:326
  153.2 1.3 collective-permute-done.3.other_ref
  154.5 13.6 %factor.1 = (f32[256,512]{1,0:T(8,128)}, f32[512,512]{1,0:T(8,128)}) custom-call(s32[2]{0:T(128)S(1)} %pad_add_fusion.scalars, f32[5,128,128]{2,1,0:T(8,128)S(1)} %bitcast.10, f32[5,128,128]{2,1,0:T(8,128)S(1)} %collective-permute-done.3.other_ref, f32[256,512]{1,0:T(8,128)S(1)} %get-tuple-element.11.residual_ref), custom_call_target="tpu_custom_call" | custom-call | tf_op jit(solution)/shard_map/factor/pallas_call | solution.py:312
  (7 shorter events, 0.1 us)
Async XLA Ops:
  1.4 1.2 copy-start
  2.6 1.0 copy-start.2
  6.8 7.3 %collective-permute-start = (f32[34,128,128]{2,1,0:T(8,128)S(1)}, f32[34,128,128]{2,1,0:T(8,128)S(1)}, u32[]{:S(2)}, u32[]{:S(2)}) collective-permute-start(f32[34,128,128]{2,1,0:T(8,128)S(1)} %get-tuple-element.8), channel_id=1, source_target_pairs={{0,1},{1,0},{2,3},{3,2},{4,5},{5,4},{6,7},{7,6},{8,9},{9,8},{10,11... | collective-permute-start | bytes 6684680 | tf_op jit(solution)/shard_map/ppermute | solution.py:326
  66.9 38.6 %copy-start.1 = (f32[256,1024]{1,0:T(8,128)S(1)}, f32[256,1024]{1,0:T(8,128)}, u32[]{:S(2)}) copy-start(f32[256,1024]{1,0:T(8,128)} %basis_ref.3) | copy-start | bytes 3145732
  66.9 38.6 %copy-start.3 = (f32[256,512]{1,0:T(8,128)S(1)}, f32[256,512]{1,0:T(8,128)}, u32[]{:S(2)}) copy-start(f32[256,512]{1,0:T(8,128)} %block_ref.3) | copy-start | bytes 1572868
  96.6 8.9 %collective-permute-start.1 = (f32[34,128,128]{2,1,0:T(8,128)S(1)}, f32[34,128,128]{2,1,0:T(8,128)S(1)}, u32[]{:S(2)}, u32[]{:S(2)}) collective-permute-start(f32[34,128,128]{2,1,0:T(8,128)S(1)} %bitcast.7), channel_id=1, source_target_pairs={{0,1},{1,0},{2,3},{3,2},{4,5},{5,4},{6,7},{7,6},{8,9},{9,8},{10,11... | collective-permute-start | bytes 6684680 | tf_op jit(solution)/shard_map/ppermute | solution.py:326
  112.2 1.7 %collective-permute-start.2 = (f32[5,128,128]{2,1,0:T(8,128)S(1)}, f32[5,128,128]{2,1,0:T(8,128)S(1)}, u32[]{:S(2)}, u32[]{:S(2)}) collective-permute-start(f32[5,128,128]{2,1,0:T(8,128)S(1)} %get-tuple-element.10), channel_id=1, source_target_pairs={{0,1},{1,0},{2,3},{3,2},{4,5},{5,4},{6,7},{7,6},{8,9},{9,8},{10,11... | collective-permute-start | bytes 983048 | tf_op jit(solution)/shard_map/ppermute | solution.py:326
  148.9 5.6 %collective-permute-start.3 = (f32[5,128,128]{2,1,0:T(8,128)S(1)}, f32[5,128,128]{2,1,0:T(8,128)S(1)}, u32[]{:S(2)}, u32[]{:S(2)}) collective-permute-start(f32[5,128,128]{2,1,0:T(8,128)S(1)} %bitcast.9), channel_id=1, source_target_pairs={{0,1},{1,0},{2,3},{3,2},{4,5},{5,4},{6,7},{7,6},{8,9},{9,8},{10,11... | collective-permute-start | bytes 983048 | tf_op jit(solution)/shard_map/ppermute | solution.py:326

commit v6 on v5

--- a/solution.py
+++ b/solution.py
@@ -335,10 +335,19 @@
     return exchange(jnp.broadcast_to(x[None], (count, *x.shape)), axes)
 
 
-def sum_halves(keep, send, near, far):
+def direct_sum(part, axis):
+    count = lax.axis_size(axis)
+    parts = [
+        lax.ppermute(part, axis, [(i, (i + d) % count) for i in range(count)])
+        for d in range(1, count)
+    ]
+    return part + sum(parts[1:], parts[0])
+
+
+def sum_halves(keep, send, near, far, direct):
     total = (keep + swap_cores(send)).reshape(lax.axis_size(near), -1, 8, 128)
     part = jnp.sum(exchange(total, near), axis=0)
-    part = jnp.sum(to_all(part, far), axis=0)
+    part = direct_sum(part, far) if direct else jnp.sum(to_all(part, far), axis=0)
     whole = to_all(part, near).reshape(keep.shape)
     return whole, swap_cores(whole)
 
@@ -357,7 +366,7 @@
         functools.partial(products_kernel, weight=weight), [half, half],
         [pltpu.VMEM((2 * tiles, BLOCK, BLOCK), jnp.float32)], "products"
     )(scalars, basis, block)
-    own, other = sum_halves(keep, send, SLAB, "grp_0")
+    own, other = sum_halves(keep, send, SLAB, "grp_0", True)
     wide = pltpu.VMEM((m * BLOCK, m * BLOCK), jnp.bfloat16)
     residual, keep, send = call(
         functools.partial(residual_kernel, weight=weight),
@@ -365,7 +374,7 @@
         [wide, wide, pltpu.VMEM((2 * gram_tiles, BLOCK, BLOCK), jnp.float32)],
         "residual",
     )(scalars, own, other, basis, block)
-    own, other = sum_halves(keep, send, PLANE, GRP)
+    own, other = sum_halves(keep, send, PLANE, GRP, False)
     new_block, factor = call(
         factor_kernel,
         [block.shape, (size, size)],

time: 168 us -> 169 us (level)
  blocking collectives: 117 us -> 105 us
  starting transfers between devices: 13 us -> 21 us
  waiting for transfers between devices: 10.5 us -> 14.6 us
    all_to_all x6 -> x5, blocking collectives: 117 us -> 105 us  [exchange(): return lax.all_to_all(x, axes, 0, 0, tiled=True)]
    ppermute x0 -> x3, starting transfers between devices: none -> 8.45 us  [direct_sum(): lax.ppermute(part, axis, [(i, (i + d) % count) for i in range(count)])]
    ppermute x0 -> x3, waiting for transfers between devices: none -> 4.09 us  [direct_sum(): lax.ppermute(part, axis, [(i, (i + d) % count) for i in range(count)])]
  transfers between devices with their start and end apart: 4 -> 7, of which waited for: 4 -> 6; matrix products, arithmetic and copies ran while one was open for 0% -> 0% of each run, Pallas kernels for 0% -> 0%
where the time goes in v6:
time: 169 us; the launch traced here: 168 us
  blocking collectives  105 us (62%)
  Pallas kernels  23.4 us (14%)
  starting transfers between devices  21 us (12%)
  waiting for transfers between devices  14.6 us (9%)
  local copies, waits for them, and re-layouts  2.46 us (1%)
    all_to_all x5, blocking collectives, exchange(): return lax.all_to_all(x, axes, 0, 0, tiled=True)  105 us
    pallas_call x3, Pallas kernels, run(): pl.pallas_call(kernel, out_shape=[jax.ShapeDtypeStruct(s, jnp.float32) fo...  23.4 us
    ppermute x4, starting transfers between devices, swap_cores(): return lax.ppermute(x, 'row_2', [(0, 1), (1, 0)])  12.6 us
    ppermute x4, waiting for transfers between devices, swap_cores(): return lax.ppermute(x, 'row_2', [(0, 1), (1, 0)])  10.5 us
    ppermute x3, starting transfers between devices, direct_sum(): lax.ppermute(part, axis, [(i, (i + d) % count) for i in range(count)])  8.45 us
    ppermute x3, waiting for transfers between devices, direct_sum(): lax.ppermute(part, axis, [(i, (i + d) % count) for i in range(count)])  4.09 us
  transfers between devices with their start and end apart: 7, of which 6 were waited for; matrix products, arithmetic and copies ran while one was open for 0% of the time, Pallas kernels for 0%

profile of v6, /device:TPU:1, one launch (start us, length us, event | category | flops | bytes accessed | tf_op | source)
XLA Modules:
  0.0 168.2 jit_solution(15232431743737981120)
XLA Ops:
  1.3 0.1 pad_add_fusion.scalars
  1.4 0.0 copy-start
  1.4 1.2 copy-done
  2.6 0.0 copy-start.2
  2.6 1.0 copy-done.2
  3.6 3.1 %products.1 = (f32[34,128,128]{2,1,0:T(8,128)S(1)}, f32[34,128,128]{2,1,0:T(8,128)S(1)}) custom-call(s32[2]{0:T(128)S(1)} %pad_add_fusion.scalars, f32[256,1024]{1,0:T(8,128)S(1)} %copy-done, f32[256,512]{1,0:T(8,128)S(1)} %copy-done.2), custom_call_target="tpu_custom_call" | custom-call | tf_op jit(solution)/shard_map/products/pallas_call | solution.py:312
  6.8 3.3 %collective-permute-start = (f32[34,128,128]{2,1,0:T(8,128)S(1)}, f32[34,128,128]{2,1,0:T(8,128)S(1)}, u32[]{:S(2)}, u32[]{:S(2)}) collective-permute-start(f32[34,128,128]{2,1,0:T(8,128)S(1)} %get-tuple-element.8), channel_id=1, source_target_pairs={{0,1},{1,0},{2,3},{3,2},{4,5},{5,4},{6,7},{7,6},{8,9},{9,8},{10,11... | collective-permute-start | bytes 6684680 | tf_op jit(solution)/shard_map/ppermute | solution.py:326
  10.1 4.0 %collective-permute-done = f32[34,128,128]{2,1,0:T(8,128)S(1)} collective-permute-done((f32[34,128,128]{2,1,0:T(8,128)S(1)}, f32[34,128,128]{2,1,0:T(8,128)S(1)}, u32[]{:S(2)}, u32[]{:S(2)}) %collective-permute-start) | collective-permute-done | bytes 2228256 | tf_op jit(solution)/shard_map/ppermute | solution.py:326
  14.1 0.3 add.15
  14.3 35.8 %all_to_all.25 = f32[32,17,8,128]{3,2,1,0:T(8,128)S(1)} all-to-all(f32[32,17,8,128]{3,2,1,0:T(8,128)S(1)} %bitcast.11), channel_id=1, replica_groups=mesh['grp_0'=4,'grp_1'=2,'row_0'=4,'row_1'=4,'row_2'=2] {'grp_1','row_0'..., dimensions={0} | all-to-all | bytes 4456448 | tf_op jit(solution)/shard_map/all_to_all | solution.py:330
  50.1 0.1 reduce_sum.27
  50.3 5.2 %collective-permute-start.3 = (f32[17,8,128]{2,1,0:T(8,128)S(1)}, f32[17,8,128]{2,1,0:T(8,128)S(1)}, u32[]{:S(2)}, u32[]{:S(2)}) collective-permute-start(f32[17,8,128]{2,1,0:T(8,128)S(1)} %reduce_sum.27), channel_id=1, source_target_pairs={{0,192},{64,0},{128,64},{192,128},{1,193},{65,1},{129,65},{193,129... | collective-permute-start | bytes 208904 | tf_op jit(solution)/shard_map/ppermute | solution.py:341
  55.4 1.2 collective-permute-start.2
  56.6 2.1 %collective-permute-start.1 = (f32[17,8,128]{2,1,0:T(8,128)S(1)}, f32[17,8,128]{2,1,0:T(8,128)S(1)}, u32[]{:S(2)}, u32[]{:S(2)}) collective-permute-start(f32[17,8,128]{2,1,0:T(8,128)S(1)} %reduce_sum.27), channel_id=1, source_target_pairs={{0,64},{64,128},{128,192},{192,0},{1,65},{65,129},{129,193},{193,1... | collective-permute-start | bytes 208904 | tf_op jit(solution)/shard_map/ppermute | solution.py:341
  58.7 0.0 collective-permute-done.3
  58.7 4.0 %collective-permute-done.2 = f32[17,8,128]{2,1,0:T(8,128)S(1)} collective-permute-done((f32[17,8,128]{2,1,0:T(8,128)S(1)}, f32[17,8,128]{2,1,0:T(8,128)S(1)}, u32[]{:S(2)}, u32[]{:S(2)}) %collective-permute-start.2) | collective-permute-done | bytes 69664 | tf_op jit(solution)/shard_map/ppermute | solution.py:341
  62.7 0.1 collective-permute-done.1
  62.8 0.1 broadcast_in_dim.6
  63.0 0.0 copy-start.1
  63.0 0.0 copy-start.3
  63.0 31.4 %all_to_all.26 = f32[32,17,8,128]{3,2,1,0:T(8,128)S(1)} all-to-all(f32[32,17,8,128]{3,2,1,0:T(8,128)S(1)} %broadcast_in_dim.6), channel_id=1, replica_groups=mesh['grp_0'=4,'grp_1'=2,'row_0'=4,'row_1'=4,'row_2'=2] {'grp_1','row_0'..., dimensions={0} | all-to-all | bytes 4456448 | tf_op jit(solution)/shard_map/all_to_all | solution.py:330
  94.4 4.5 %collective-permute-start.4 = (f32[34,128,128]{2,1,0:T(8,128)S(1)}, f32[34,128,128]{2,1,0:T(8,128)S(1)}, u32[]{:S(2)}, u32[]{:S(2)}) collective-permute-start(f32[34,128,128]{2,1,0:T(8,128)S(1)} %bitcast.7), channel_id=1, source_target_pairs={{0,1},{1,0},{2,3},{3,2},{4,5},{5,4},{6,7},{7,6},{8,9},{9,8},{10,11... | collective-permute-start | bytes 6684680 | tf_op jit(solution)/shard_map/ppermute | solution.py:326
  98.9 4.0 %collective-permute-done.4.other_ref = f32[34,128,128]{2,1,0:T(8,128)S(1)} collective-permute-done((f32[34,128,128]{2,1,0:T(8,128)S(1)}, f32[34,128,128]{2,1,0:T(8,128)S(1)}, u32[]{:S(2)}, u32[]{:S(2)}) %collective-permute-start.4) | collective-permute-done | bytes 2228256 | tf_op jit(solution)/shard_map/ppermute | solution.py:326
  102.8 0.0 copy-done.1
  102.8 0.0 copy-done.3
  102.8 6.7 %residual.1 = (f32[256,512]{1,0:T(8,128)S(1)}, f32[5,128,128]{2,1,0:T(8,128)S(1)}, f32[5,128,128]{2,1,0:T(8,128)S(1)}) custom-call(s32[2]{0:T(128)S(1)} %pad_add_fusion.scalars, f32[34,128,128]{2,1,0:T(8,128)S(1)} %bitcast.8, f32[34,128,128]{2,1,0:T(8,128)S(1)} %collective-permute-done.4.other_ref, f32[256,1024]{1,0:T(8,128)S(1)} %copy-done.1, ...), custom_call_target="tpu_custom_call" | custom-call | tf_op jit(solution)/shard_map/residual/pallas_call | solution.py:312
  109.6 0.5 collective-permute-start.5
  110.0 1.3 collective-permute-done.5
  111.3 11.0 %all_to_all.27 = f32[16,5,8,128]{3,2,1,0:T(8,128)S(1)} all-to-all(f32[16,5,8,128]{3,2,1,0:T(8,128)S(1)} %bitcast.12), channel_id=1, replica_groups=mesh['grp_0'=4,'grp_1'=2,'row_0'=4,'row_1'=4,'row_2'=2] {'row_0','row_1'}, dimensions={0} | all-to-all | bytes 655360 | tf_op jit(solution)/shard_map/all_to_all | solution.py:330
  122.3 15.2 %all_to_all.28 = f32[8,5,8,128]{3,2,1,0:T(8,128)S(1)} all-to-all(f32[8,5,8,128]{3,2,1,0:T(8,128)S(1)} %broadcast_in_dim.7), channel_id=1, replica_groups=mesh['grp_0'=4,'grp_1'=2,'row_0'=4,'row_1'=4,'row_2'=2] {'grp_0','grp_1'}, dimensions={0} | all-to-all | bytes 327680 | tf_op jit(solution)/shard_map/all_to_all | solution.py:330
  137.6 11.5 %all_to_all.29 = f32[16,5,8,128]{3,2,1,0:T(8,128)S(1)} all-to-all(f32[16,5,8,128]{3,2,1,0:T(8,128)S(1)} %broadcast_in_dim.8), channel_id=1, replica_groups=mesh['grp_0'=4,'grp_1'=2,'row_0'=4,'row_1'=4,'row_2'=2] {'row_0','row_1'}, dimensions={0} | all-to-all | bytes 655360 | tf_op jit(solution)/shard_map/all_to_all | solution.py:330
  149.1 4.3 %collective-permute-start.6 = (f32[5,128,128]{2,1,0:T(8,128)S(1)}, f32[5,128,128]{2,1,0:T(8,128)S(1)}, u32[]{:S(2)}, u32[]{:S(2)}) collective-permute-start(f32[5,128,128]{2,1,0:T(8,128)S(1)} %bitcast.9), channel_id=1, source_target_pairs={{0,1},{1,0},{2,3},{3,2},{4,5},{5,4},{6,7},{7,6},{8,9},{9,8},{10,11... | collective-permute-start | bytes 983048 | tf_op jit(solution)/shard_map/ppermute | solution.py:326
  153.4 1.3 collective-permute-done.6.other_ref
  154.7 13.6 %factor.1 = (f32[256,512]{1,0:T(8,128)}, f32[512,512]{1,0:T(8,128)}) custom-call(s32[2]{0:T(128)S(1)} %pad_add_fusion.scalars, f32[5,128,128]{2,1,0:T(8,128)S(1)} %bitcast.10, f32[5,128,128]{2,1,0:T(8,128)S(1)} %collective-permute-done.6.other_ref, f32[256,512]{1,0:T(8,128)S(1)} %get-tuple-element.11.residual_ref), custom_call_target="tpu_custom_call" | custom-call | tf_op jit(solution)/shard_map/factor/pallas_call | solution.py:312
  (6 shorter events, 0.1 us)
Async XLA Ops:
  1.4 1.2 copy-start
  2.6 1.0 copy-start.2
  6.8 7.3 %collective-permute-start = (f32[34,128,128]{2,1,0:T(8,128)S(1)}, f32[34,128,128]{2,1,0:T(8,128)S(1)}, u32[]{:S(2)}, u32[]{:S(2)}) collective-permute-start(f32[34,128,128]{2,1,0:T(8,128)S(1)} %get-tuple-element.8), channel_id=1, source_target_pairs={{0,1},{1,0},{2,3},{3,2},{4,5},{5,4},{6,7},{7,6},{8,9},{9,8},{10,11... | collective-permute-start | bytes 6684680 | tf_op jit(solution)/shard_map/ppermute | solution.py:326
  50.3 8.5 %collective-permute-start.3 = (f32[17,8,128]{2,1,0:T(8,128)S(1)}, f32[17,8,128]{2,1,0:T(8,128)S(1)}, u32[]{:S(2)}, u32[]{:S(2)}) collective-permute-start(f32[17,8,128]{2,1,0:T(8,128)S(1)} %reduce_sum.27), channel_id=1, source_target_pairs={{0,192},{64,0},{128,64},{192,128},{1,193},{65,1},{129,65},{193,129... | collective-permute-start | bytes 208904 | tf_op jit(solution)/shard_map/ppermute | solution.py:341
  55.4 7.3 %collective-permute-start.2 = (f32[17,8,128]{2,1,0:T(8,128)S(1)}, f32[17,8,128]{2,1,0:T(8,128)S(1)}, u32[]{:S(2)}, u32[]{:S(2)}) collective-permute-start(f32[17,8,128]{2,1,0:T(8,128)S(1)} %reduce_sum.27), channel_id=1, source_target_pairs={{0,128},{64,192},{128,0},{192,64},{1,129},{65,193},{129,1},{193,65... | collective-permute-start | bytes 208904 | tf_op jit(solution)/shard_map/ppermute | solution.py:341
  56.6 6.2 %collective-permute-start.1 = (f32[17,8,128]{2,1,0:T(8,128)S(1)}, f32[17,8,128]{2,1,0:T(8,128)S(1)}, u32[]{:S(2)}, u32[]{:S(2)}) collective-permute-start(f32[17,8,128]{2,1,0:T(8,128)S(1)} %reduce_sum.27), channel_id=1, source_target_pairs={{0,64},{64,128},{128,192},{192,0},{1,65},{65,129},{129,193},{193,1... | collective-permute-start | bytes 208904 | tf_op jit(solution)/shard_map/ppermute | solution.py:341
  63.0 39.9 %copy-start.1 = (f32[256,1024]{1,0:T(8,128)S(1)}, f32[256,1024]{1,0:T(8,128)}, u32[]{:S(2)}) copy-start(f32[256,1024]{1,0:T(8,128)} %basis_ref.3) | copy-start | bytes 3145732
  63.0 39.9 %copy-start.3 = (f32[256,512]{1,0:T(8,128)S(1)}, f32[256,512]{1,0:T(8,128)}, u32[]{:S(2)}) copy-start(f32[256,512]{1,0:T(8,128)} %block_ref.3) | copy-start | bytes 1572868
  94.4 8.4 %collective-permute-start.4 = (f32[34,128,128]{2,1,0:T(8,128)S(1)}, f32[34,128,128]{2,1,0:T(8,128)S(1)}, u32[]{:S(2)}, u32[]{:S(2)}) collective-permute-start(f32[34,128,128]{2,1,0:T(8,128)S(1)} %bitcast.7), channel_id=1, source_target_pairs={{0,1},{1,0},{2,3},{3,2},{4,5},{5,4},{6,7},{7,6},{8,9},{9,8},{10,11... | collective-permute-start | bytes 6684680 | tf_op jit(solution)/shard_map/ppermute | solution.py:326
  109.6 1.7 %collective-permute-start.5 = (f32[5,128,128]{2,1,0:T(8,128)S(1)}, f32[5,128,128]{2,1,0:T(8,128)S(1)}, u32[]{:S(2)}, u32[]{:S(2)}) collective-permute-start(f32[5,128,128]{2,1,0:T(8,128)S(1)} %get-tuple-element.10), channel_id=1, source_target_pairs={{0,1},{1,0},{2,3},{3,2},{4,5},{5,4},{6,7},{7,6},{8,9},{9,8},{10,11... | collective-permute-start | bytes 983048 | tf_op jit(solution)/shard_map/ppermute | solution.py:326
  149.1 5.6 %collective-permute-start.6 = (f32[5,128,128]{2,1,0:T(8,128)S(1)}, f32[5,128,128]{2,1,0:T(8,128)S(1)}, u32[]{:S(2)}, u32[]{:S(2)}) collective-permute-start(f32[5,128,128]{2,1,0:T(8,128)S(1)} %bitcast.9), channel_id=1, source_target_pairs={{0,1},{1,0},{2,3},{3,2},{4,5},{5,4},{6,7},{7,6},{8,9},{9,8},{10,11... | collective-permute-start | bytes 983048 | tf_op jit(solution)/shard_map/ppermute | solution.py:326
